TPU v7x, 128 devices: a whole 4x4x4 slice. The times are simulated.
128 devices in a mesh: coef: 8 (over z, core), track: 16 (over y, x).
Axes of the slice: x: 4, y: 4, z: 4, core: 2. Of those that a mesh axis runs over, the one named last changes fastest.
Arguments:
- probes: bfloat16 [2, 640, 128, 1200], P(None, 'coef', 'track'), may hold values from -6 to 6
- legendre: bfloat16 [640, 64, 1200], P('coef'), may hold values from -0.1875 to 0.1875
- order_map: int32 [640], replicated, may hold values from 0 to 639, each once
- tile_index: int32 [8, 16, 24], P('coef'), may hold values from 0 to 79
- tile_count: int32 [8, 16], P('coef'), may hold values from 1 to 24, 192 in all within a row
- base_offset: int32 [8, 16, 24, 512], P('coef', 'track'), may hold values from 0 to 127
- stencil_weight: bfloat16 [8, 16, 24, 4, 512], P('coef', 'track'), may hold values from -0.5 to 1.5
- obs_weight: float32 [8, 16, 24, 512], P('coef', 'track'), may hold values from 0.1 to 10
Outputs:
- panel: float32 [2, 640, 128, 1200], P(None, ('coef', 'track'))
- factor: float32 [128, 128], replicated
Inputs may be any that keep to these rules, and one draw needn't show every extreme that they name: `tile_count`: in each coef row the counts sum to 192; slots of an owner at or past its count are unused. `order_map`: each order appears in exactly one slot.
All inputs are finite; a program needn't handle non-finite values.
Results may differ from a plain program's by a relative error of at most 0.0045.
Values may be sent and summed in bfloat16 or wider, within the bound.
A program may use at most 128 MiB of HBM per device.

v0:
```python
import math

import jax
import jax.numpy as jnp
from jax import lax
from jax.sharding import PartitionSpec as P

NDEG = 1200
ORDERS = 640
NLON = 1280


HIGHEST = lax.Precision.HIGHEST


def trig_tables(order_slots):
    longitude = jnp.arange(NLON, dtype=jnp.int32)
    phase = order_slots[:, None] * longitude[None, :] % NLON
    angle = phase.astype(jnp.float32) * jnp.float32(2.0 * math.pi / NLON)
    scale = jnp.float32(1.0 / math.sqrt(ORDERS))
    tables = jnp.stack([jnp.cos(angle) * scale, jnp.sin(angle) * scale])
    return tables.reshape(2, order_slots.shape[0], NLON // 128, 128)


def stencil_matrix(base, weights):
    points = jnp.arange(128, dtype=jnp.int32)
    summed = jnp.zeros(base.shape + (128,), jnp.float32)
    for i in range(4):
        matches = (((base + i) % 128)[..., None] == points).astype(jnp.float32)
        summed = summed + weights[..., i, :, None].astype(jnp.float32) * matches
    return summed.astype(jnp.bfloat16)


def on_device(
    probes, legendre, order_map, tile_index, tile_count, base_offset, stencil_weight, obs_weight
):
    coef_index = lax.axis_index("coef")
    track_index = lax.axis_index("track")
    order_block = probes.shape[1]
    every_table = trig_tables(order_map)
    lat_coef = jnp.einsum("cmpl,mal->cmpa", probes, legendre, preferred_element_type=jnp.float32)
    my_orders = lax.dynamic_slice_in_dim(order_map, coef_index * order_block, order_block)
    local_tables = trig_tables(my_orders)
    grid = lax.psum_scatter(
        jnp.einsum("cmpa,cmbq->abpq", lat_coef, local_tables, precision=HIGHEST),
        "coef",
        scatter_dimension=0,
        tiled=True,
    )
    tiles = grid.astype(jnp.bfloat16).reshape(grid.shape[0] * grid.shape[1], grid.shape[2], 128)
    index_rows = tile_index[0]
    outgoing = tiles[index_rows]
    incoming = lax.all_to_all(outgoing, "track", split_axis=0, concat_axis=2, tiled=True)[0]
    stencil = stencil_matrix(base_offset[0, 0], stencil_weight[0, 0])
    values = jnp.einsum("soq,spq->sop", stencil, incoming, preferred_element_type=jnp.float32)
    count_here = lax.dynamic_index_in_dim(tile_count[0], track_index, keepdims=False)
    live = (jnp.arange(stencil.shape[0], dtype=jnp.int32) < count_here).astype(jnp.float32)
    resid = (values * obs_weight[0, 0][:, :, None] * live[:, None, None]).astype(jnp.bfloat16)
    adjoint = jnp.einsum("soq,sop->spq", stencil, resid, preferred_element_type=jnp.float32).astype(
        jnp.bfloat16
    )
    returned = lax.all_to_all(adjoint[None], "track", split_axis=2, concat_axis=0, tiled=True)
    selector = (index_rows[..., None] == jnp.arange(tiles.shape[0], dtype=jnp.int32)).astype(
        jnp.bfloat16
    )
    summed = jnp.einsum("tsj,tspq->jpq", selector, returned, preferred_element_type=jnp.float32)
    adjoint_grid = summed.reshape(grid.shape)
    spectra = jnp.einsum("cmbq,abpq->cmpa", every_table, adjoint_grid, precision=HIGHEST)
    spectra_band = lax.all_to_all(
        spectra.astype(jnp.bfloat16), "coef", split_axis=1, concat_axis=3, tiled=True
    ).astype(spectra.dtype)
    rounded = spectra_band.astype(jnp.bfloat16)
    spectra_rows = lax.all_to_all(rounded, "track", split_axis=1, concat_axis=2, tiled=True)
    own_count = spectra_rows.shape[1]
    own_table = lax.dynamic_slice_in_dim(legendre, track_index * own_count, own_count, 0)
    panel_rows = jnp.einsum(
        "cmpa,mal->cmpl", spectra_rows, own_table, preferred_element_type=jnp.float32
    )
    gram_part = jnp.einsum("cmpl,cmql->pq", panel_rows, panel_rows, precision=HIGHEST)
    gram = lax.psum(gram_part, ("coef", "track")) / (2 * ORDERS * NDEG)
    lower = jnp.linalg.cholesky(gram)
    inverse = jax.scipy.linalg.solve_triangular(
        lower, jnp.eye(gram.shape[0], dtype=jnp.float32), lower=True
    )
    panel = jnp.einsum("pq,cmql->cmpl", inverse, panel_rows, precision=HIGHEST)
    return (panel, lower.T)


def solution(mesh):
    return jax.shard_map(
        on_device,
        mesh=mesh,
        in_specs=(
            P(None, "coef", "track", None),
            P("coef", None, None),
            P(),
            P("coef", None, None),
            P("coef", None),
            P("coef", "track", None, None),
            P("coef", "track", None, None, None),
            P("coef", "track", None, None),
        ),
        out_specs=(P(None, ("coef", "track"), None, None), P()),
        check_vma=False,
    )
```

profile of v0, /device:TPU:1, one launch (start us, length us, event | category | flops | bytes accessed | tf_op | source)
XLA Modules:
  0.0 409.4 jit_solution(11420529780917545407)
XLA Ops:
  9.1 8.2 %fusion.25 = f32[2,80,8,64]{3,2,0,1:T(8,128)} fusion(bf16[2,80,8,1200]{3,2,1,0:T(8,128)(2,1)S(1)} %copy-done, bf16[80,64,1200]{2,1,0:T(8,128)(2,1)} %param.9), kind=kOutput, calls=%fused_computation.36 | convolution fusion | flops 196608000 | bytes 15687680 | tf_op jit(solution)/shard_map/cmpl,mal->cmpa/dot_general | solution.py:41
  21.3 4.8 %convolution_bitcast_fusion.1 = f32[64,10,8,128]{3,0,2,1:T(8,128)} fusion(f32[1,80,10,128]{3,1,0,2:T(8,128)S(1)} %get-tuple-element.23, f32[1,80,10,128]{3,1,0,2:T(8,128)S(1)} %get-tuple-element.22, f32[2,80,8,64]{1,3,0,2:T(8,128)} %copy.49), kind=kOutput, calls=%fused_computation.33 | convolution fusion | flops 1258496000 | bytes 3768320 | tf_op jit(solution)/shard_map/cmpa,cmbq->abpq/dot_general | solution.py:45
  27.7 33.8 %reduce-scatter.2.cloned.1.call-done = f32[8,10,8,128]{3,0,2,1:T(8,128)} async-done(((f32[64,10,8,128]{3,0,2,1:T(8,128)}), f32[8,10,8,128]{3,0,2,1:T(8,128)}) %reduce-scatter.2.cloned.1.call-update) | async-done | bytes 327696 | tf_op jit(solution)/shard_map/reduce_scatter | solution.py:44
  62.6 2.3 gather_fusion
  64.8 6.7 %all-to-all-start = ((bf16[16,24,8,128]{3,2,1,0:T(8,128)(2,1)}), bf16[16,24,8,128]{3,2,1,0:T(8,128)(2,1)}, u32[]{:S(2)}, u32[]{:S(2)}) async-start(bf16[16,24,8,128]{3,2,1,0:T(8,128)(2,1)} %bitcast.160), calls=%async_computation.1 | async-start | bytes 1572864 | tf_op jit(solution)/shard_map/all_to_all | solution.py:53
  75.1 6.9 %all-to-all-done = bf16[16,24,8,128]{3,2,1,0:T(8,128)(2,1)} async-done(((bf16[16,24,8,128]{3,2,1,0:T(8,128)(2,1)}), bf16[16,24,8,128]{3,2,1,0:T(8,128)(2,1)}, u32[]{:S(2)}, u32[]{:S(2)}) %all-to-all-start) | async-done | bytes 786464 | tf_op jit(solution)/shard_map/all_to_all | solution.py:53
  82.1 19.6 %multiply_convert_fusion.9 = bf16[24,512,128]{2,1,0:T(8,128)(2,1)S(1)} fusion(f32[24]{0:T(128)S(1)} %compare_convert_fusion, f32[24,512]{1,0:T(8,128)} %bitcast.166, f32[24,512]{1,0:T(8,128)S(1)} %get-tuple-element.24, s32[24,512]{1,0:T(8,128)} %get-tuple-element.17, f32[24,512]{1,0:T(8,128)} %get-tuple-element.25, ...), kind=kOutput, calls=%fused_computation.7.clone.clone.clone.clone.clone.clone.2 | convolution fusion | flops 426246144 | bytes 4374624 | tf_op jit(solution)/shard_map/soq,spq->sop/dot_general | solution.py:55
  101.7 19.9 %fusion.24 = bf16[1,24,128,128]{3,2,1,0:T(8,128)(2,1)S(1)} fusion(f32[24,512]{1,0:T(8,128)S(1)} %get-tuple-element.24, s32[24,512]{1,0:T(8,128)S(1)} %copy-done.4, f32[24,512]{1,0:T(8,128)S(1)} %copy-done.3, s32[24,512]{1,0:T(8,128)S(1)} %copy-done.5, f32[24,512]{1,0:T(8,128)S(1)} %get-tuple-element.26, s32[24,512]{1,0:T(8,128)S(1)} %copy-done.6, ...), kind=kOutput, calls=%fused_computation.35 | convolution fusion | flops 421920768 | bytes 4325376 | tf_op jit(solution)/shard_map/soq,sop->spq/dot_general | solution.py:59
  123.0 4.5 %all-to-all-start.1 = ((bf16[1,24,128,128]{3,1,0,2:T(8,128)(2,1)}), bf16[1,24,128,128]{3,1,0,2:T(8,128)(2,1)}, u32[]{:S(2)}, u32[]{:S(2)}) async-start(bf16[1,24,128,128]{3,1,0,2:T(8,128)(2,1)} %copy.53), calls=%async_computation.2 | async-start | bytes 1572864 | tf_op jit(solution)/shard_map/all_to_all | solution.py:62
  127.5 15.1 %cosine_multiply_fusion = (f32[1,640,10,128]{3,1,2,0:T(8,128)}, f32[1,640,10,128]{3,1,2,0:T(8,128)}) fusion(s32[10,128]{1,0:T(8,128)S(1)} %multiply_add_fusion, s32[640]{0:T(1024)S(1)} %copy-done.9), kind=kLoop, calls=%fused_computation.24 | loop fusion | flops 9011200 | bytes 6561280 | tf_op jit(solution)/shard_map/mul | solution.py:21
  144.3 8.6 %fusion.32 = bf16[2,640,8,8]{1,2,0,3:T(8,128)(2,1)S(1)} fusion(f32[1,640,10,128]{3,1,2,0:T(8,128)} %get-tuple-element.21, f32[1,640,10,128]{3,1,2,0:T(8,128)} %get-tuple-element.20, f32[8,10,8,128,1]{3,1,2,0,4:T(8,128)S(1)} %convolution_bitcast_fusion.2), kind=kOutput, calls=%fused_computation.40 | convolution fusion | flops 1260011520 | bytes 7045120 | tf_op jit(solution)/shard_map/cmbq,abpq->cmpa/dot_general | solution.py:68
  152.9 4.0 copy.57
  157.0 8.0 %reshape.337 = bf16[8,2,5120]{2,1,0:T(2,128)(2,1)S(1)} reshape(bf16[640,8,2,8]{3,2,1,0:T(2,128)(2,1)} %bitcast.157) | data formatting | bytes 327680
  165.0 16.9 %all_to_all.69 = bf16[8,2,5120]{2,1,0:T(2,128)(2,1)} all-to-all(bf16[8,2,5120]{2,1,0:T(2,128)(2,1)S(1)} %reshape.337), channel_id=1, replica_groups=mesh['coef'=8,'track'=16] {'coef'}, dimensions={0} | all-to-all | bytes 327680 | tf_op jit(solution)/shard_map/all_to_all | solution.py:69
  181.9 9.3 %reshape.338 = bf16[640,8,2,8]{3,2,1,0:T(2,128)(2,1)} reshape(bf16[8,2,5120]{2,1,0:T(2,128)(2,1)} %all_to_all.69) | data formatting | bytes 327680
  191.2 5.5 %copy.87 = bf16[2,8,80,8,8]{2,4,1,3,0:T(8,128)(2,1)S(1)} copy(bf16[2,8,80,8,8]{3,0,4,2,1:T(2,128)(2,1)} %bitcast.158) | data formatting | bytes 327680 | tf_op jit(solution)/shard_map/all_to_all | solution.py:69
  199.6 7.0 %all-to-all-start.3 = ((bf16[16,2,2560]{2,1,0:T(2,128)(2,1)}), bf16[16,2,2560]{2,1,0:T(2,128)(2,1)S(1)}, u32[]{:S(2)}, u32[]{:S(2)}) async-start(bf16[16,2,2560]{2,1,0:T(2,128)(2,1)} %reshape.339), calls=%async_computation.4 | async-start | bytes 327680 | tf_op jit(solution)/shard_map/all_to_all | solution.py:73
  206.8 6.7 %all-to-all-done.3 = bf16[16,2,2560]{2,1,0:T(2,128)(2,1)S(1)} async-done(((bf16[16,2,2560]{2,1,0:T(2,128)(2,1)}), bf16[16,2,2560]{2,1,0:T(2,128)(2,1)S(1)}, u32[]{:S(2)}, u32[]{:S(2)}) %all-to-all-start.3) | async-done | bytes 163872 | tf_op jit(solution)/shard_map/all_to_all | solution.py:73
  216.8 2.6 copy-done.1
  219.4 10.7 %fusion.33 = f32[128,128]{0,1:T(8,128)} fusion(f32[2,5,128,1200]{2,3,0,1:T(8,128)S(1)} %convolution_bitcast_fusion), kind=kOutput, calls=%fused_computation.41 | convolution fusion | flops 2359296000 | bytes 6209536 | tf_op jit(solution)/shard_map/cmpl,cmql->pq/dot_general | solution.py:79
  230.1 137.3 %all-reduce.2.cloned.1.call-done = f32[128,128]{0,1:T(8,128)} async-done(((f32[128,128]{0,1:T(8,128)}), f32[128,128]{0,1:T(8,128)}) %all-reduce.2.cloned.1.call-update) | async-done | bytes 65552 | tf_op jit(solution)/shard_map/psum | solution.py:80
  369.3 12.0 %cholesky.17 = f32[128,128]{1,0:T(8,128)S(1)} custom-call(f32[128,128]{1,0:T(8,128)S(1)} %fusion.59), custom_call_target="Cholesky" | custom-call | tf_op jit(solution)/shard_map/jit(cholesky)/cholesky | solution.py:81
  383.3 9.8 %custom-call.7 = f32[1,128,128]{1,2,0:T(8,128)S(1)} custom-call(f32[1,128,128]{2,1,0:T(8,128)S(1)} %get-tuple-element.15), custom_call_target="InvertDiagBlocksLowerTriangular" | custom-call | tf_op jit(solution)/shard_map/jit(_solve_triangular)/triangular_solve | solution.py:82
  393.4 8.7 %fusion.9 = f32[2,5,128,1200]{2,3,1,0:T(8,128)} fusion(f32[128,128,1,1]{1,0,3,2:T(8,128)S(1)} %convolution_bitcast_fusion.3, f32[2,5,128,1200]{2,3,0,1:T(8,128)} %copy-done.1), kind=kOutput, calls=%fused_computation.18 | convolution fusion | flops 2359296000 | bytes 12353536 | tf_op jit(solution)/shard_map/pq,cmql->cmpl/dot_general | solution.py:85
  (56 shorter events, 25.6 us)
Async XLA Ops:
  7.2 1.9 copy-start
  7.2 54.3 %reduce-scatter.2.cloned.1.call-start = ((), (), s32[]{:S(2)}) async-start(), calls=%async_computation.5 | async-start | bytes 2949120 | tf_op jit(solution)/shard_map/reduce_scatter | solution.py:44
  9.1 10.4 %copy-start.9 = (s32[640]{0:T(1024)S(1)}, s32[640]{0:T(1024)}, u32[]{:S(2)}) copy-start(s32[640]{0:T(1024)} %param.10) | copy-start | bytes 7684
  17.3 8.9 %copy-start.7 = (s32[1,16,24]{2,1,0:T(8,128)S(1)}, s32[1,16,24]{2,1,0:T(8,128)}, u32[]{:S(2)}) copy-start(s32[1,16,24]{2,1,0:T(8,128)} %param.11) | copy-start | bytes 4612
  17.3 9.0 %copy-start.10 = (s32[1,16]{1,0:T(1,128)S(1)}, s32[1,16]{1,0:T(1,128)}, u32[]{:S(2)}) copy-start(s32[1,16]{1,0:T(1,128)} %param.12) | copy-start | bytes 196
  17.3 9.6 %copy-start.2 = (bf16[1,1,24,4,512]{4,3,2,1,0:T(4,128)(2,1)S(1)}, bf16[1,1,24,4,512]{4,3,2,1,0:T(4,128)(2,1)}, u32[]{:S(2)}) copy-start(bf16[1,1,24,4,512]{4,3,2,1,0:T(4,128)(2,1)} %param.14) | copy-start | bytes 294916
  64.8 17.2 %all-to-all-start = ((bf16[16,24,8,128]{3,2,1,0:T(8,128)(2,1)}), bf16[16,24,8,128]{3,2,1,0:T(8,128)(2,1)}, u32[]{:S(2)}, u32[]{:S(2)}) async-start(bf16[16,24,8,128]{3,2,1,0:T(8,128)(2,1)} %bitcast.160), calls=%async_computation.1 | async-start | bytes 1572864 | tf_op jit(solution)/shard_map/all_to_all | solution.py:53
  82.0 19.6 %copy-start.3 = (f32[24,512]{1,0:T(8,128)S(1)}, f32[24,512]{1,0:T(8,128)}, u32[]{:S(2)}) copy-start(f32[24,512]{1,0:T(8,128)} %get-tuple-element.25) | copy-start | bytes 147460
  82.1 19.6 %copy-start.4 = (s32[24,512]{1,0:T(8,128)S(1)}, s32[24,512]{1,0:T(8,128)}, u32[]{:S(2)}) copy-start(s32[24,512]{1,0:T(8,128)} %get-tuple-element.17) | copy-start | bytes 147460
  82.1 19.7 %copy-start.5 = (s32[24,512]{1,0:T(8,128)S(1)}, s32[24,512]{1,0:T(8,128)}, u32[]{:S(2)}) copy-start(s32[24,512]{1,0:T(8,128)} %get-tuple-element.18) | copy-start | bytes 147460
  82.1 19.7 %copy-start.6 = (s32[24,512]{1,0:T(8,128)S(1)}, s32[24,512]{1,0:T(8,128)}, u32[]{:S(2)}) copy-start(s32[24,512]{1,0:T(8,128)} %get-tuple-element.19) | copy-start | bytes 147460
  121.6 21.0 %copy-start.8 = (s32[1,16,24]{2,1,0:T(8,128)S(1)}, s32[1,16,24]{2,1,0:T(8,128)}, u32[]{:S(2)}) copy-start(s32[1,16,24]{2,1,0:T(8,128)} %param.11) | copy-start | bytes 4612
  123.0 19.6 %all-to-all-start.1 = ((bf16[1,24,128,128]{3,1,0,2:T(8,128)(2,1)}), bf16[1,24,128,128]{3,1,0,2:T(8,128)(2,1)}, u32[]{:S(2)}, u32[]{:S(2)}) async-start(bf16[1,24,128,128]{3,1,0,2:T(8,128)(2,1)} %copy.53), calls=%async_computation.2 | async-start | bytes 1572864 | tf_op jit(solution)/shard_map/all_to_all | solution.py:62
  199.6 14.0 %all-to-all-start.3 = ((bf16[16,2,2560]{2,1,0:T(2,128)(2,1)}), bf16[16,2,2560]{2,1,0:T(2,128)(2,1)S(1)}, u32[]{:S(2)}, u32[]{:S(2)}) async-start(bf16[16,2,2560]{2,1,0:T(2,128)(2,1)} %reshape.339), calls=%async_computation.4 | async-start | bytes 327680 | tf_op jit(solution)/shard_map/all_to_all | solution.py:73
  206.5 160.9 %all-reduce.2.cloned.1.call-start = ((), (), s32[]{:S(2)}) async-start(), calls=%async_computation.6 | async-start | bytes 131072 | tf_op jit(solution)/shard_map/psum | solution.py:80
  216.8 2.6 copy-start.1
Sparse Core Ops, SparseCore 0:
  26.3 35.2 reduce-scatter.1
  230.3 137.1 all-reduce.1
where the time goes:
time: 417 us; the launch traced here: 409 us
  waiting for transfers between devices  185 us (44%)
  matrix products  84.7 us (20%)
  other arithmetic  45.6 us (11%)
  local copies, waits for them, and re-layouts  44.2 us (11%)
  starting transfers between devices  18.4 us (4%)
  blocking collectives  16.9 us (4%)
  between operations  14.7 us (4%)
    psum x1, waiting for transfers between devices, on_device(): gram = lax.psum(gram_part, ('coef', 'track')) / (2 * ORDERS * NDEG)  137 us
    reduce_scatter x1, waiting for transfers between devices, on_device(): lax.psum_scatter(jnp.einsum('cmpa,cmbq->abpq', lat_coef, local_tables, pr...  33.8 us
    unnamed x29, local copies, waits for them, and re-layouts  26.8 us
    dot_general x1, matrix products, on_device(): jnp.einsum('soq,sop->spq', stencil, resid, preferred_element_type=jnp.flo...  19.9 us
    dot_general x1, matrix products, on_device(): jnp.einsum('soq,spq->sop', stencil, incoming, preferred_element_type=jnp....  19.6 us
    all_to_all x1, blocking collectives, on_device(): lax.all_to_all(spectra.astype(jnp.bfloat16), 'coef', split_axis=1, concat...  16.9 us
    mul x2, other arithmetic, trig_tables(): tables = jnp.stack([jnp.cos(angle) * scale, jnp.sin(angle) * scale])  16.9 us
    another operation x3, other arithmetic, on_device(): lower = jnp.linalg.cholesky(gram)  12.6 us
  transfers between devices with their start and end apart: 5, of which 4 were waited for; matrix products, arithmetic and copies ran while one was open for 5% of the time, Pallas kernels for 0%

commit v1 on v0

v1 whole, which is shorter than its diff:
```python
import math

import jax
import jax.numpy as jnp
from jax import lax
from jax.experimental import pallas as pl
from jax.experimental.pallas import tpu as pltpu
from jax.sharding import PartitionSpec as P

NDEG = 1200
ORDERS = 640
NLON = 1280
NC = 8
NT = 16
ND = NC * NT
OWN = 5
UNITS = 40
PIECE = 3

BF = jnp.bfloat16
F32 = jnp.float32
HIGHEST = lax.Precision.HIGHEST
MESH = pl.DeviceIdType.MESH
VM = pl.BlockSpec(memory_space=pltpu.VMEM)
SM = pl.BlockSpec(memory_space=pltpu.SMEM)


def mm(a, b):
    return lax.dot_general(a, b, (((1,), (0,)), ((), ())), preferred_element_type=F32)


def mm_nt(a, b):
    return lax.dot_general(a, b, (((1,), (1,)), ((), ())), preferred_element_type=F32)


def mm_tn(a, b):
    return lax.dot_general(a, b, (((0,), (0,)), ((), ())), preferred_element_type=F32)


def split(x):
    hi = x.astype(BF)
    return hi, (x - hi.astype(F32)).astype(BF)


def normal_kernel(index_ref, count_ref, base_ref, coef_ref, weight_ref, out_ref, prod_ref, diag_ref):
    slots, obs = base_ref.shape
    live = lax.broadcasted_iota(jnp.int32, (slots, obs), 0) < count_ref[0]
    weight = jnp.where(live, weight_ref[...], 0.0)
    row = 0
    for d in range(4):
        for i in range(4 - d):
            left = coef_ref[:, i, :].astype(F32)
            right = coef_ref[:, i + d, :].astype(F32)
            prod_ref[:, row, :] = left * right * weight
            row += 1
    points = lax.broadcasted_iota(jnp.int32, (128, obs), 0)

    def slot(s, carry):
        hot = jnp.where(points == base_ref[pl.ds(s, 1), :], 1.0, 0.0).astype(BF)
        full = prod_ref[s]
        hi, mid = split(full)
        low = (full - hi.astype(F32) - mid.astype(F32)).astype(BF)
        hist = mm_nt(hi, hot) + mm_nt(mid, hot) + mm_nt(low, hot)
        row = 0
        for d in range(4):
            total = hist[row : row + 1, :]
            row += 1
            for i in range(1, 4 - d):
                total = total + pltpu.roll(hist[row : row + 1, :], i, axis=1)
                row += 1
            diag_ref[s, d : d + 1, :] = total
        return carry

    prod_ref[:, 10:16, :] = jnp.zeros((slots, 6, obs), F32)
    lax.fori_loop(0, slots, slot, 0)
    rows = lax.broadcasted_iota(jnp.int32, (80, slots), 0)
    tile = (rows % 8) * 10 + rows // 8
    pick = jnp.where(tile == index_ref[...], 1.0, 0.0).astype(F32)
    tables = [
        lax.dot_general(
            pick, diag_ref[:, d, :], (((1,), (0,)), ((), ())), precision=HIGHEST, preferred_element_type=F32
        )
        for d in range(4)
    ]
    for u in range(NT * PIECE):
        if u < UNITS:
            b, d = u // 4, u % 4
            block = tables[d][b * 8 : (b + 1) * 8, :]
        else:
            block = jnp.zeros((8, 128), F32)
        out_ref[u // PIECE, u % PIECE] = block


def normal_tables(index_row, count, base, coef, weight):
    slots, obs = base.shape
    return pl.pallas_call(
        normal_kernel,
        name="normal_tables",
        out_shape=jax.ShapeDtypeStruct((NT, PIECE, 8, 128), F32),
        in_specs=[VM, SM, VM, VM, VM],
        out_specs=VM,
        scratch_shapes=[pltpu.VMEM((slots, 16, obs), F32), pltpu.VMEM((slots, 4, 128), F32)],
    )(index_row, count, base, coef, weight)


def exchange_kernel(
    lat_ref, norm_ref, lat_out, norm_out, part, lat_send, lat_recv, rs_send, rs_recv, ag_send, ag_recv
):
    c = lax.axis_index("coef")
    t = lax.axis_index("track")
    barrier = pltpu.get_barrier_semaphore()
    for i in range(1, NC):
        pl.semaphore_signal(barrier, 1, device_id=((c + i) % NC, t), device_id_type=MESH)
    for i in range(1, NT):
        pl.semaphore_signal(barrier, 1, device_id=(c, (t + i) % NT), device_id_type=MESH)
    pl.semaphore_wait(barrier, NC + NT - 2)

    def lat_copy(i):
        peer = (c + i) % NC
        return pltpu.make_async_remote_copy(
            lat_ref.at[peer], lat_out.at[c], lat_send, lat_recv, device_id=(peer, t), device_id_type=MESH
        )

    def rs_copy(i):
        peer = (t + i) % NT
        return pltpu.make_async_remote_copy(
            norm_ref.at[peer], part.at[t], rs_send, rs_recv, device_id=(c, peer), device_id_type=MESH
        )

    def ag_copy(i):
        peer = (t + i) % NT
        return pltpu.make_async_remote_copy(
            norm_out.at[t], norm_out.at[t], ag_send, ag_recv, device_id=(c, peer), device_id_type=MESH
        )

    for i in range(1, NT):
        rs_copy(i).start()
    for i in range(1, NC):
        lat_copy(i).start()
    lat_out[c] = lat_ref[c]
    part[t] = norm_ref[t]
    pltpu.make_async_copy(part.at[pl.ds(0, NT - 1)], part.at[pl.ds(0, NT - 1)], rs_recv).wait()
    total = part[0]
    for s in range(1, NT):
        total = total + part[s]
    norm_out[t] = total
    for i in range(1, NT):
        ag_copy(i).start()
    pltpu.make_async_copy(lat_out.at[pl.ds(0, NC - 1)], lat_out.at[pl.ds(0, NC - 1)], lat_recv).wait()
    pltpu.make_async_copy(norm_out.at[pl.ds(0, NT - 1)], norm_out.at[pl.ds(0, NT - 1)], ag_recv).wait()
    pltpu.make_async_copy(part.at[pl.ds(0, NT - 1)], part.at[pl.ds(0, NT - 1)], rs_send).wait()
    pltpu.make_async_copy(lat_ref.at[pl.ds(0, NC - 1)], lat_ref.at[pl.ds(0, NC - 1)], lat_send).wait()
    pltpu.make_async_copy(norm_out.at[pl.ds(0, NT - 1)], norm_out.at[pl.ds(0, NT - 1)], ag_send).wait()


def exchange(lat, norm):
    return pl.pallas_call(
        exchange_kernel,
        name="exchange",
        out_shape=(jax.ShapeDtypeStruct(lat.shape, lat.dtype), jax.ShapeDtypeStruct(norm.shape, norm.dtype)),
        in_specs=[VM, VM],
        out_specs=(VM, VM),
        scratch_shapes=[pltpu.VMEM(norm.shape, F32)] + [pltpu.SemaphoreType.DMA] * 6,
        compiler_params=pltpu.CompilerParams(collective_id=0, has_side_effects=True),
    )(lat, norm)


def grid_kernel(lat_ref, norm_ref, trig_ref, out_ref, hi_ref, lo_ref, adj_ref, spec_ref, turn_ref):
    def make(j, carry):
        cos_q, sin_q, cos_b, sin_b = (trig_ref[k, pl.ds(j * 128, 128), :] for k in range(4))
        for b in range(10):
            ca, sa = cos_b[:, b : b + 1], sin_b[:, b : b + 1]
            cols = slice(b * 128, (b + 1) * 128)
            hi, lo = split(ca * cos_q - sa * sin_q)
            hi_ref[j, :, cols] = hi
            lo_ref[j, :, cols] = lo
            hi, lo = split(sa * cos_q + ca * sin_q)
            hi_ref[OWN + j, :, cols] = hi
            lo_ref[OWN + j, :, cols] = lo
        return carry

    lax.fori_loop(0, OWN, make, 0)
    grid = jnp.zeros((64, NLON), F32)
    for s in range(NC):
        rows = slice(s * NT, (s + 1) * NT)
        grid = grid + mm(lat_ref[s], hi_ref[:, rows, :].reshape(160, NLON))
        grid = grid + mm(lat_ref[s], lo_ref[:, rows, :].reshape(160, NLON))
    for b in range(10):
        x = grid[:, b * 128 : (b + 1) * 128]

        def diagonal(d):
            unit = b * 4 + d
            block = norm_ref[unit // PIECE, unit % PIECE]
            return jnp.broadcast_to(block[None], (8, 8, 128)).reshape(64, 128)

        adj = diagonal(0) * x
        for d in range(1, 4):
            m = diagonal(d)
            adj = adj + m * pltpu.roll(x, 128 - d, axis=1) + pltpu.roll(m * x, d, axis=1)
        hi, lo = split(adj)
        adj_ref[:64, b * 128 : (b + 1) * 128] = hi
        adj_ref[64:, b * 128 : (b + 1) * 128] = lo
    for i in range(10):
        both = mm_nt(adj_ref[...], hi_ref[i])
        spec_ref[i] = both[:64] + both[64:] + mm_nt(adj_ref[:64, :], lo_ref[i])
    spec_ref[10:] = jnp.zeros((6, 64, 128), F32)
    for p in range(8):
        block = spec_ref[:, p * 8 : (p + 1) * 8, :].reshape(128, 128)
        turn_ref[pl.ds(p, 128, stride=8), :] = block.T
    out_ref[...] = turn_ref[...].reshape(128, 8, 128).astype(BF)


def grid_stage(lat, norm, trig):
    return pl.pallas_call(
        grid_kernel,
        name="grid_stage",
        out_shape=jax.ShapeDtypeStruct((ND, 8, 128), BF),
        in_specs=[VM, VM, VM],
        out_specs=VM,
        scratch_shapes=[
            pltpu.VMEM((10, 128, NLON), BF),
            pltpu.VMEM((10, 128, NLON), BF),
            pltpu.VMEM((128, NLON), BF),
            pltpu.VMEM((16, 64, 128), F32),
            pltpu.VMEM((1024, 128), F32),
        ],
        compiler_params=pltpu.CompilerParams(vmem_limit_bytes=48 * 1024 * 1024),
    )(lat, norm, trig)


def gram_kernel(
    spec_ref, leg_ref, rows_out, gram_out, recv, perm, normal, g_part, g_coef, g_track,
    a_send, a_recv, b_send, b_recv, c_send, c_recv, d_send, d_recv,
):
    c = lax.axis_index("coef")
    t = lax.axis_index("track")
    me = c * NT + t
    barrier = pltpu.get_barrier_semaphore()

    def greet(i, carry):
        peer = (me + i) % ND
        pl.semaphore_signal(barrier, 1, device_id=(peer // NT, peer % NT), device_id_type=MESH)
        return carry

    lax.fori_loop(1, ND, greet, 0)
    pl.semaphore_wait(barrier, ND - 1)

    def send(i, carry):
        peer = (me + i) % ND
        pltpu.make_async_remote_copy(
            spec_ref.at[peer], recv.at[me], a_send, a_recv,
            device_id=(peer // NT, peer % NT), device_id_type=MESH,
        ).start()
        return carry

    lax.fori_loop(1, ND, send, 0)
    recv[me] = spec_ref[me]
    same = (lax.broadcasted_iota(jnp.int32, (128, 128), 0) < 64) == (
        lax.broadcasted_iota(jnp.int32, (128, 128), 1) < 64
    )
    for j in range(OWN):
        one = leg_ref[j]
        two = jnp.concatenate([one, one], axis=0)
        hi, lo = split(jnp.where(same, mm_nt(two, two), 0.0))
        normal[0, j] = hi
        normal[1, j] = lo
    row = lax.broadcasted_iota(jnp.int32, (1024, 640), 0)
    col = lax.broadcasted_iota(jnp.int32, (1024, 640), 1)
    src_band, src_i, src_a = row // 128, (row % 128) // 8, row % 8
    dst_j, dst_half, dst_band, dst_a = col // 128, (col % 128) // 64, (col % 64) // 8, col % 8
    hit = (src_band == dst_band) & (src_a == dst_a) & (src_i == dst_half * OWN + dst_j)
    perm[...] = jnp.where(hit, 1.0, 0.0).astype(BF)
    pltpu.make_async_copy(recv.at[pl.ds(0, ND - 1)], recv.at[pl.ds(0, ND - 1)], a_recv).wait()
    gathered = jnp.zeros((128, 640), F32)
    for s in range(NC):
        block = recv[s * NT : (s + 1) * NT].astype(F32).reshape(128, 128).astype(BF)
        gathered = gathered + mm(block, perm[s * 128 : (s + 1) * 128, :])
    gram = jnp.zeros((128, 128), F32)
    for j in range(OWN):
        rows = gathered[:, j * 128 : (j + 1) * 128].astype(BF)
        rows_out[j] = rows
        hi, lo = split(mm(rows, normal[0, j]) + mm(rows, normal[1, j]))
        gram = gram + mm_nt(hi, rows) + mm_nt(lo, rows)
    g_part[...] = gram.reshape(NC, 16, 128)

    def to_coef(ref, dst, sems, peer):
        return pltpu.make_async_remote_copy(ref, dst, *sems, device_id=(peer, t), device_id_type=MESH)

    for i in range(1, NC):
        peer = (c + i) % NC
        to_coef(g_part.at[peer], g_coef.at[c], (b_send, b_recv), peer).start()
    g_coef[c] = g_part[c]
    pltpu.make_async_copy(g_coef.at[pl.ds(0, NC - 1)], g_coef.at[pl.ds(0, NC - 1)], b_recv).wait()
    total = g_coef[0]
    for s in range(1, NC):
        total = total + g_coef[s]
    g_track[t] = total
    for i in range(1, NT):
        peer = (t + i) % NT
        pltpu.make_async_remote_copy(
            g_track.at[t], g_track.at[t], c_send, c_recv, device_id=(c, peer), device_id_type=MESH
        ).start()
    pltpu.make_async_copy(g_track.at[pl.ds(0, NT - 1)], g_track.at[pl.ds(0, NT - 1)], c_recv).wait()
    total = g_track[0]
    for s in range(1, NT):
        total = total + g_track[s]
    gram_out[c] = total * (1.0 / (2 * ORDERS * NDEG))
    for i in range(1, NC):
        peer = (c + i) % NC
        to_coef(gram_out.at[c], gram_out.at[c], (d_send, d_recv), peer).start()
    pltpu.make_async_copy(gram_out.at[pl.ds(0, NC - 1)], gram_out.at[pl.ds(0, NC - 1)], d_recv).wait()
    pltpu.make_async_copy(recv.at[pl.ds(0, ND - 1)], recv.at[pl.ds(0, ND - 1)], a_send).wait()
    pltpu.make_async_copy(g_part.at[pl.ds(0, NC - 1)], g_part.at[pl.ds(0, NC - 1)], b_send).wait()
    pltpu.make_async_copy(g_track.at[pl.ds(0, NT - 1)], g_track.at[pl.ds(0, NT - 1)], c_send).wait()
    pltpu.make_async_copy(gram_out.at[pl.ds(0, NC - 1)], gram_out.at[pl.ds(0, NC - 1)], d_send).wait()


def gram_stage(spec, own_table):
    return pl.pallas_call(
        gram_kernel,
        name="gram_stage",
        out_shape=(jax.ShapeDtypeStruct((OWN, 128, 128), BF), jax.ShapeDtypeStruct((NC, 16, 128), F32)),
        in_specs=[VM, VM],
        out_specs=(VM, VM),
        scratch_shapes=[
            pltpu.VMEM((ND, 8, 128), BF),
            pltpu.VMEM((1024, 640), BF),
            pltpu.VMEM((2, OWN, 128, 128), BF),
            pltpu.VMEM((NC, 16, 128), F32),
            pltpu.VMEM((NC, 16, 128), F32),
            pltpu.VMEM((NT, 16, 128), F32),
        ]
        + [pltpu.SemaphoreType.DMA] * 8,
        compiler_params=pltpu.CompilerParams(collective_id=1, has_side_effects=True),
    )(spec, own_table)


def panel_kernel(inv_ref, rows_ref, leg_ref, out_ref):
    hi, lo = split(inv_ref[...])
    z = mm(hi, rows_ref[0]) + mm(lo, rows_ref[0])
    z_hi, z_lo = split(z)
    left = lax.broadcasted_iota(jnp.int32, (128, 128), 1) < 64
    hi_f, lo_f = z_hi.astype(F32), z_lo.astype(F32)
    cosine = jnp.where(left, hi_f, pltpu.roll(lo_f, 64, axis=1)).astype(BF)
    sine = jnp.where(left, pltpu.roll(hi_f, 64, axis=1), lo_f).astype(BF)
    one = leg_ref[0]
    two = jnp.concatenate([one, one], axis=0)
    contract = (((0,), (1,)), ((), ()))
    out_ref[0, 0] = lax.dot_general(two, cosine, contract, preferred_element_type=F32)
    out_ref[1, 0] = lax.dot_general(two, sine, contract, preferred_element_type=F32)


def panel_stage(inverse, rows, own_table):
    return pl.pallas_call(
        panel_kernel,
        name="panel_stage",
        grid=(OWN,),
        out_shape=jax.ShapeDtypeStruct((2, OWN, NDEG, 128), F32),
        in_specs=[
            pl.BlockSpec((128, 128), lambda j: (0, 0)),
            pl.BlockSpec((1, 128, 128), lambda j: (j, 0, 0)),
            pl.BlockSpec((1, 64, NDEG), lambda j: (j, 0, 0)),
        ],
        out_specs=pl.BlockSpec((2, 1, NDEG, 128), lambda j: (0, j, 0, 0)),
    )(inverse, rows, own_table)


def trig_factors(order_map):
    order = order_map.reshape(NC, NT, OWN).transpose(2, 0, 1).reshape(ORDERS, 1)
    lane = jnp.arange(128, dtype=jnp.int32)[None, :]
    unit = F32(2.0 * math.pi / NLON)
    point = (order * lane % NLON).astype(F32) * unit
    offset = (order * (lane * 128) % NLON).astype(F32) * unit
    scale = F32(1.0 / math.sqrt(ORDERS))
    return jnp.stack([jnp.cos(point), jnp.sin(point), jnp.cos(offset) * scale, jnp.sin(offset) * scale])


def on_device(
    probes, legendre, order_map, tile_index, tile_count, base_offset, stencil_weight, obs_weight
):
    t = lax.axis_index("track")
    lat = jnp.einsum("cmpl,mal->mcpa", probes, legendre, preferred_element_type=F32)
    lat = lat.reshape(NT, OWN, 2, 8, NC, 8).transpose(4, 3, 5, 2, 1, 0)
    lat = lat.astype(BF).reshape(NC, 64, 160)
    index_row = lax.dynamic_slice_in_dim(tile_index[0], t, 1, 0)
    count = lax.dynamic_slice_in_dim(tile_count[0], t, 1, 0)
    norm = normal_tables(index_row, count, base_offset[0, 0], stencil_weight[0, 0], obs_weight[0, 0])
    lat, norm = exchange(lat, norm)
    spec = grid_stage(lat, norm, trig_factors(order_map))
    own_table = lax.dynamic_slice_in_dim(legendre, t * OWN, OWN, 0)
    rows, gram = gram_stage(spec, own_table)
    lower = jnp.linalg.cholesky(gram.reshape(128, 128))
    inverse = jax.scipy.linalg.solve_triangular(lower, jnp.eye(128, dtype=F32), lower=True)
    panel = panel_stage(inverse, rows, own_table)
    return (jnp.swapaxes(panel, 2, 3), lower.T)


def solution(mesh):
    return jax.shard_map(
        on_device,
        mesh=mesh,
        in_specs=(
            P(None, "coef", "track", None),
            P("coef", None, None),
            P(),
            P("coef", None, None),
            P("coef", None),
            P("coef", "track", None, None),
            P("coef", "track", None, None, None),
            P("coef", "track", None, None),
        ),
        out_specs=(P(None, ("coef", "track"), None, None), P()),
        check_vma=False,
    )
```

time: 417 us -> 130 us (0.31); the launches traced: 409 us -> 130 us
  waiting for transfers between devices: 185 us -> 0 us
  matrix products: 84.7 us -> 10.1 us
  Pallas kernels: 0 us -> 71.9 us
  local copies, waits for them, and re-layouts: 44.2 us -> 20.3 us
  other arithmetic: 45.6 us -> 26.5 us
  starting transfers between devices: 18.4 us -> 0 us
  blocking collectives: 16.9 us -> 0 us
  between operations: 14.7 us -> 0.74 us
    psum x1 -> x0, waiting for transfers between devices: 137 us -> none  [on_device(): gram = lax.psum(gram_part, ('coef', 'track')) / (2 * ORDERS * NDEG)]
    dot_general x9 -> x1, matrix products: 84.5 us -> 9.21 us  [on_device(): jnp.einsum('cmpl,mal->mcpa', probes, legendre, preferred_element_type=F32)]
    pallas_call x0 -> x5, Pallas kernels: none -> 71.9 us  [the longest x1 31.8 us: gram_stage(): pl.pallas_call(gram_kernel, name='gram_stage', out_shape=(jax.ShapeDtypeS...]
    reduce_scatter x1 -> x0, waiting for transfers between devices: 33.8 us -> none  [on_device(): lax.psum_scatter(jnp.einsum('cmpa,cmbq->abpq', lat_coef, local_tables, pr...]
    unnamed x29 -> x9, local copies, waits for them, and re-layouts: 26.8 us -> 3.31 us
    all_to_all x3 -> x0, starting transfers between devices: 18.1 us -> none  [the longest x1 6.97 us: on_device(): lax.all_to_all(rounded, 'track', split_axis=1, concat_axis=2, tiled=True)]
    all_to_all x1 -> x0, blocking collectives: 16.9 us -> none  [on_device(): lax.all_to_all(spectra.astype(jnp.bfloat16), 'coef', split_axis=1, concat...]
    mul x3 -> x1, other arithmetic: 16.9 us -> 0.01 us  [trig_factors(): offset = (order * (lane * 128) % NLON).astype(F32) * unit]
  transfers between devices with their start and end apart: 5 -> 0, of which waited for: 4 -> 0; matrix products, arithmetic and copies ran while one was open for 5% -> 0% of each run, Pallas kernels for 0% -> 0%
where the time goes in v1:
time: 130 us
  Pallas kernels  71.9 us (55%)
  other arithmetic  26.5 us (20%)
  local copies, waits for them, and re-layouts  20.3 us (16%)
  matrix products  10.1 us (8%)
    pallas_call x1, Pallas kernels, gram_stage(): pl.pallas_call(gram_kernel, name='gram_stage', out_shape=(jax.ShapeDtypeS...  31.8 us
    pallas_call x1, Pallas kernels, exchange(): pl.pallas_call(exchange_kernel, name='exchange', out_shape=(jax.ShapeDtyp...  17.8 us
    another operation x3, other arithmetic, on_device(): lower = jnp.linalg.cholesky(gram.reshape(128, 128))  12.4 us
    pallas_call x1, Pallas kernels, normal_tables(): pl.pallas_call(normal_kernel, name='normal_tables', out_shape=jax.ShapeDt...  10.1 us
    another operation x1, other arithmetic, on_device(): jax.scipy.linalg.solve_triangular(lower, jnp.eye(128, dtype=F32), lower=T...  9.81 us
    dot_general x1, matrix products, on_device(): jnp.einsum('cmpl,mal->mcpa', probes, legendre, preferred_element_type=F32)  9.21 us
    convert_element_type x2, local copies, waits for them, and re-layouts, on_device(): lat = lat.astype(BF).reshape(NC, 64, 160)  8.83 us
    pallas_call x1, Pallas kernels, panel_stage(): pl.pallas_call(panel_kernel, name='panel_stage', grid=(OWN,), out_shape=j...  6.46 us

profile of v1, /device:TPU:1, one launch (start us, length us, event | category | flops | bytes accessed | tf_op | source)
XLA Modules:
  0.0 129.6 jit_solution(2951056871432069671)
XLA Ops:
  0.6 1.2 constant_dynamic-slice_fusion.1
  2.4 0.9 reshape.272
  3.5 10.1 %normal_tables.1.norm_ref = f32[16,3,8,128]{3,2,1,0:T(8,128)} custom-call(s32[1,24]{1,0:T(1,128)} %fusion.24.index_ref, s32[1]{0:T(128)} %bitcast.4.count_ref, s32[24,512]{1,0:T(8,128)} %bitcast.36, bf16[24,4,512]{2,1,0:T(4,128)(2,1)} %bitcast.35, f32[24,512]{1,0:T(8,128)} %bitcast.37), custom_call_target="tpu_custom_call" | custom-call | tf_op jit(solution)/shard_map/normal_tables/pallas_call | solution.py:96
  13.6 9.2 %fusion.3 = bf16[80,2,8,64]{3,2,1,0:T(8,128)(2,1)S(1)} fusion(bf16[80,64,1200]{2,1,0:T(8,128)(2,1)} %param.9, bf16[2,80,8,1200]{3,2,1,0:T(8,128)(2,1)} %param.8), kind=kOutput, calls=%fused_computation.4 | convolution fusion | flops 196689920 | bytes 15523840 | tf_op jit(solution)/shard_map/cmpl,mal->mcpa/dot_general | solution.py:382
  22.8 2.1 %constant_dynamic-slice_fusion.leg_ref = bf16[5,64,1200]{2,1,0:T(8,128)(2,1)} fusion(bf16[80,64,1200]{2,1,0:T(8,128)(2,1)} %param.9, s32[]{:T(128)S(6)} %select_n.47), kind=kLoop, calls=%fused_computation.34 | loop fusion | bytes 1536004 | tf_op jit(solution)/shard_map/dynamic_slice | solution.py:390
  24.9 2.7 %fusion.17 = (f32[1,640,128]{2,1,0:T(8,128)S(1)}, f32[1,640,128]{2,1,0:T(8,128)S(1)}, f32[1,640,128]{2,1,0:T(8,128)S(1)}, f32[1,640,128]{2,1,0:T(8,128)S(1)}) fusion(s32[640]{0:T(1024)S(1)} %mul.110, s32[128]{0:T(128)S(1)} %iota_multiply_fusion), kind=kLoop, calls=%fused_computation.20 | loop fusion | flops 1638400 | bytes 1313792 | tf_op jit(solution)/shard_map/cos | solution.py:375
  27.7 2.7 %convert_element_type.39 = bf16[16,5,2,8,8,8]{5,4,3,2,1,0:T(8,128)(2,1)} reshape(bf16[80,2,8,64]{3,2,1,0:T(8,128)(2,1)S(1)} %fusion.3) | data formatting | bytes 327680 | tf_op jit(solution)/shard_map/convert_element_type | solution.py:384
  30.4 6.1 %copy.16 = bf16[8,8,8,2,5,16]{5,4,3,2,1,0:T(8,128)(2,1)S(1)} copy(bf16[8,8,8,2,5,16]{2,0,1,3,4,5:T(8,128)(2,1)} %bitcast.31) | data formatting | bytes 327680 | tf_op jit(solution)/shard_map/convert_element_type | solution.py:384
  36.5 2.3 %reshape.271.lat_ref = bf16[8,64,160]{2,1,0:T(8,128)(2,1)} reshape(bf16[8,8,8,2,5,16]{5,4,3,2,1,0:T(8,128)(2,1)S(1)} %copy.16) | data formatting | bytes 327680 | tf_op jit(solution)/shard_map/reshape | solution.py:384
  38.8 17.8 %exchange.1 = (bf16[8,64,160]{2,1,0:T(8,128)(2,1)}, f32[16,3,8,128]{3,2,1,0:T(8,128)}) custom-call(bf16[8,64,160]{2,1,0:T(8,128)(2,1)} %reshape.271.lat_ref, f32[16,3,8,128]{3,2,1,0:T(8,128)} %normal_tables.1.norm_ref), custom_call_target="tpu_custom_call" | custom-call | tf_op jit(solution)/shard_map/exchange/pallas_call | solution.py:157
  56.6 0.9 copy-done.2
  57.6 0.9 copy-done.3
  58.5 5.9 %grid_stage.1.spec_ref = bf16[128,8,128]{2,1,0:T(8,128)(2,1)S(1)} custom-call(bf16[8,64,160]{2,1,0:T(8,128)(2,1)S(1)} %copy-done.2, f32[16,3,8,128]{3,2,1,0:T(8,128)S(1)} %copy-done.3, f32[4,640,128]{2,1,0:T(8,128)S(1)} %pad_maximum_fusion.trig_ref), custom_call_target="tpu_custom_call" | custom-call | tf_op jit(solution)/shard_map/grid_stage/pallas_call | solution.py:214
  64.4 0.7 copy-done.1
  65.1 31.8 %gram_stage.1 = (bf16[5,128,128]{2,1,0:T(8,128)(2,1)}, f32[8,16,128]{2,1,0:T(8,128)}) custom-call(bf16[128,8,128]{2,1,0:T(8,128)(2,1)} %copy-done.1, bf16[5,64,1200]{2,1,0:T(8,128)(2,1)} %constant_dynamic-slice_fusion.leg_ref), custom_call_target="tpu_custom_call" | custom-call | tf_op jit(solution)/shard_map/gram_stage/pallas_call | solution.py:319
  96.8 0.9 copy.18
  97.8 0.9 fusion.22
  98.6 11.7 %cholesky.17 = f32[128,128]{1,0:T(8,128)S(1)} custom-call(f32[128,128]{1,0:T(8,128)S(1)} %fusion.22), custom_call_target="Cholesky" | custom-call | tf_op jit(solution)/shard_map/jit(cholesky)/cholesky | solution.py:392
  110.4 0.6 compare_reduce_fusion
  111.0 0.7 fusion.23
  111.7 0.7 copy.19
  112.4 9.8 %custom-call.7 = f32[1,128,128]{1,2,0:T(8,128)S(1)} custom-call(f32[1,128,128]{2,1,0:T(8,128)S(1)} %get-tuple-element.15), custom_call_target="InvertDiagBlocksLowerTriangular" | custom-call | tf_op jit(solution)/shard_map/jit(_solve_triangular)/triangular_solve | solution.py:393
  122.2 0.9 fusion.20.inv_ref
  123.1 6.5 %panel_stage.1 = f32[2,5,1200,128]{3,2,1,0:T(8,128)} custom-call(f32[128,128]{1,0:T(8,128)} %fusion.20.inv_ref, bf16[5,128,128]{2,1,0:T(8,128)(2,1)} %get-tuple-element.9.rows_ref, bf16[5,64,1200]{2,1,0:T(8,128)(2,1)} %constant_dynamic-slice_fusion.leg_ref), custom_call_target="tpu_custom_call" | custom-call | tf_op jit(solution)/shard_map/panel_stage/pallas_call | solution.py:354
  (11 shorter events, 0.9 us)
Async XLA Ops:
  0.6 1.3 copy-start
  56.6 1.0 copy-start.2
  57.6 0.9 copy-start.3
  64.4 0.7 copy-start.1

commit v2 on v1

--- a/solution.py
+++ b/solution.py
@@ -335,7 +335,58 @@
     )(spec, own_table)
 
 
-def panel_kernel(inv_ref, rows_ref, leg_ref, out_ref):
+def exact(a, b, dims):
+    return lax.dot_general(a, b, (dims, ((), ())), precision=HIGHEST, preferred_element_type=F32)
+
+
+NN = ((1,), (0,))
+NT_DIMS = ((1,), (1,))
+
+
+def factorize(gram, upper_ref, inv_ref):
+    n = gram.shape[0]
+    row = lax.broadcasted_iota(jnp.int32, (n, n), 0)
+    col = lax.broadcasted_iota(jnp.int32, (n, n), 1)
+    eye = jnp.where(row == col, 1.0, 0.0)
+    half = jnp.where(row > col, 1.0, 0.5 * eye)
+    diag = jnp.where(row == col, gram, 0.0)
+    r_col = lax.rsqrt(jnp.sum(diag, axis=1, keepdims=True))
+    r_row = lax.rsqrt(jnp.sum(diag, axis=0, keepdims=True))
+    inverse = (eye - half * (gram * r_col * r_row - eye)) * r_row
+    error = eye
+    for _ in range(3):
+        error = exact(exact(inverse, gram, NN), inverse, NT_DIMS) - eye
+        inverse = inverse - exact(half * error, inverse, NN)
+    inv_ref[...] = inverse
+    upper_ref[...] = jnp.where(row <= col, exact(inverse, gram, NN), 0.0)
+    worst = jnp.max(jnp.abs(error))
+
+    @pl.when(jnp.logical_not(worst < 1e-4))
+    def _():
+        def column(j, state):
+            left, upper, inv = state
+            at_row, at_col = row == j, col == j
+            line = jnp.sum(jnp.where(at_row, left, 0.0), axis=0, keepdims=True)
+            down = jnp.sum(jnp.where(at_col, left, 0.0), axis=1, keepdims=True)
+            pivot = jnp.sum(jnp.where(at_row & at_col, left, 0.0), keepdims=True)
+            scale = 1.0 / jnp.sqrt(pivot)
+            line = jnp.where(col[:1] >= j, line * scale, 0.0)
+            below = jnp.where(row[:, :1] > j, down * scale, 0.0)
+            inv_line = jnp.sum(jnp.where(at_row, inv, 0.0), axis=0, keepdims=True) * scale
+            inv = jnp.where(at_row, inv_line, inv - below * inv_line)
+            upper = jnp.where(at_row, line, upper)
+            return left - below * line, upper, inv
+
+        _, upper, inv = lax.fori_loop(0, n, column, (gram, jnp.zeros_like(gram), eye))
+        upper_ref[...] = upper
+        inv_ref[...] = inv
+
+
+def panel_kernel(gram_ref, rows_ref, leg_ref, out_ref, upper_ref, inv_ref):
+    @pl.when(pl.program_id(0) == 0)
+    def _():
+        factorize(gram_ref[...].reshape(128, 128), upper_ref, inv_ref)
+
     hi, lo = split(inv_ref[...])
     z = mm(hi, rows_ref[0]) + mm(lo, rows_ref[0])
     z_hi, z_lo = split(z)
@@ -350,19 +401,26 @@
     out_ref[1, 0] = lax.dot_general(two, sine, contract, preferred_element_type=F32)
 
 
-def panel_stage(inverse, rows, own_table):
+def panel_stage(gram, rows, own_table):
     return pl.pallas_call(
         panel_kernel,
         name="panel_stage",
         grid=(OWN,),
-        out_shape=jax.ShapeDtypeStruct((2, OWN, NDEG, 128), F32),
+        out_shape=(
+            jax.ShapeDtypeStruct((2, OWN, NDEG, 128), F32),
+            jax.ShapeDtypeStruct((128, 128), F32),
+        ),
         in_specs=[
-            pl.BlockSpec((128, 128), lambda j: (0, 0)),
+            pl.BlockSpec((NC, 16, 128), lambda j: (0, 0, 0)),
             pl.BlockSpec((1, 128, 128), lambda j: (j, 0, 0)),
             pl.BlockSpec((1, 64, NDEG), lambda j: (j, 0, 0)),
         ],
-        out_specs=pl.BlockSpec((2, 1, NDEG, 128), lambda j: (0, j, 0, 0)),
-    )(inverse, rows, own_table)
+        out_specs=(
+            pl.BlockSpec((2, 1, NDEG, 128), lambda j: (0, j, 0, 0)),
+            pl.BlockSpec((128, 128), lambda j: (0, 0)),
+        ),
+        scratch_shapes=[pltpu.VMEM((128, 128), F32)],
+    )(gram, rows, own_table)
 
 
 def trig_factors(order_map):
@@ -389,10 +447,8 @@
     spec = grid_stage(lat, norm, trig_factors(order_map))
     own_table = lax.dynamic_slice_in_dim(legendre, t * OWN, OWN, 0)
     rows, gram = gram_stage(spec, own_table)
-    lower = jnp.linalg.cholesky(gram.reshape(128, 128))
-    inverse = jax.scipy.linalg.solve_triangular(lower, jnp.eye(128, dtype=F32), lower=True)
-    panel = panel_stage(inverse, rows, own_table)
-    return (jnp.swapaxes(panel, 2, 3), lower.T)
+    panel, upper = panel_stage(gram, rows, own_table)
+    return (jnp.swapaxes(panel, 2, 3), upper)
 
 
 def solution(mesh):

time: 130 us -> 106 us (0.82)
  other arithmetic: 26.5 us -> 2.81 us
  Pallas kernels: 71.9 us -> 74.4 us
  local copies, waits for them, and re-layouts: 20.3 us -> 18.6 us
    another operation x4 -> x0, other arithmetic: 22.2 us -> none  [the longest x3 12.4 us: on_device(): lower = jnp.linalg.cholesky(gram.reshape(128, 128))]
    pallas_call x1, Pallas kernels: 6.46 us -> 8.89 us  [panel_stage(): pl.pallas_call(panel_kernel, name='panel_stage', grid=(OWN,), out_shape=(...]
    unnamed x9 -> x8, local copies, waits for them, and re-layouts: 3.31 us -> 2.58 us
where the time goes in v2:
time: 106 us
  Pallas kernels  74.4 us (70%)
  local copies, waits for them, and re-layouts  18.6 us (18%)
  matrix products  9.21 us (9%)
  other arithmetic  2.81 us (3%)
    pallas_call x1, Pallas kernels, gram_stage(): pl.pallas_call(gram_kernel, name='gram_stage', out_shape=(jax.ShapeDtypeS...  31.8 us
    pallas_call x1, Pallas kernels, exchange(): pl.pallas_call(exchange_kernel, name='exchange', out_shape=(jax.ShapeDtyp...  17.8 us
    pallas_call x1, Pallas kernels, normal_tables(): pl.pallas_call(normal_kernel, name='normal_tables', out_shape=jax.ShapeDt...  10.1 us
    dot_general x1, matrix products, on_device(): jnp.einsum('cmpl,mal->mcpa', probes, legendre, preferred_element_type=F32)  9.21 us
    pallas_call x1, Pallas kernels, panel_stage(): pl.pallas_call(panel_kernel, name='panel_stage', grid=(OWN,), out_shape=(...  8.89 us
    convert_element_type x2, local copies, waits for them, and re-layouts, on_device(): lat = lat.astype(BF).reshape(NC, 64, 160)  8.83 us
    pallas_call x1, Pallas kernels, grid_stage(): pl.pallas_call(grid_kernel, name='grid_stage', out_shape=jax.ShapeDtypeSt...  5.84 us
    cos x1, other arithmetic, trig_factors(): jnp.cos(point)  2.72 us

profile of v2, /device:TPU:1, one launch (start us, length us, event | category | flops | bytes accessed | tf_op | source)
XLA Modules:
  0.0 105.7 jit_solution(9364330554640498933)
XLA Ops:
  0.6 0.0 copy-start
  0.6 1.2 %constant_dynamic-slice_fusion.1 = s32[1,1]{1,0:T(1,128)} fusion(s32[1,16]{1,0:T(1,128)} %param.12, s32[]{:T(128)S(6)} %select_n.40), kind=kLoop, calls=%fused_computation.24 | loop fusion | bytes 12 | tf_op jit(solution)/shard_map/dynamic_slice | solution.py:444
  1.9 0.0 copy-done
  1.9 0.5 fusion.20.index_ref
  2.4 0.9 reshape.259
  3.3 0.1 copy.14
  3.4 0.1 mul.110
  3.5 10.1 %normal_tables.1.norm_ref = f32[16,3,8,128]{3,2,1,0:T(8,128)} custom-call(s32[1,24]{1,0:T(1,128)} %fusion.20.index_ref, s32[1]{0:T(128)} %bitcast.4.count_ref, s32[24,512]{1,0:T(8,128)} %bitcast.21, bf16[24,4,512]{2,1,0:T(4,128)(2,1)} %bitcast.20, f32[24,512]{1,0:T(8,128)} %bitcast.22), custom_call_target="tpu_custom_call" | custom-call | tf_op jit(solution)/shard_map/normal_tables/pallas_call | solution.py:96
  13.6 9.2 %fusion.3 = bf16[80,2,8,64]{3,2,1,0:T(8,128)(2,1)S(1)} fusion(bf16[80,64,1200]{2,1,0:T(8,128)(2,1)} %param.9, bf16[2,80,8,1200]{3,2,1,0:T(8,128)(2,1)} %param.8), kind=kOutput, calls=%fused_computation.4 | convolution fusion | flops 196689920 | bytes 15523840 | tf_op jit(solution)/shard_map/cmpl,mal->mcpa/dot_general | solution.py:440
  22.8 2.1 %constant_dynamic-slice_fusion.leg_ref = bf16[5,64,1200]{2,1,0:T(8,128)(2,1)} fusion(bf16[80,64,1200]{2,1,0:T(8,128)(2,1)} %param.9, s32[]{:T(128)S(6)} %select_n.43), kind=kLoop, calls=%fused_computation.23 | loop fusion | bytes 1536004 | tf_op jit(solution)/shard_map/dynamic_slice | solution.py:448
  24.9 2.7 %fusion.17 = (f32[1,640,128]{2,1,0:T(8,128)S(1)}, f32[1,640,128]{2,1,0:T(8,128)S(1)}, f32[1,640,128]{2,1,0:T(8,128)S(1)}, f32[1,640,128]{2,1,0:T(8,128)S(1)}) fusion(s32[640]{0:T(1024)S(1)} %mul.110, s32[128]{0:T(128)S(1)} %iota_multiply_fusion), kind=kLoop, calls=%fused_computation.20 | loop fusion | flops 1638400 | bytes 1313792 | tf_op jit(solution)/shard_map/cos | solution.py:433
  27.6 0.1 pad_maximum_fusion.trig_ref
  27.7 2.7 %convert_element_type.38 = bf16[16,5,2,8,8,8]{5,4,3,2,1,0:T(8,128)(2,1)} reshape(bf16[80,2,8,64]{3,2,1,0:T(8,128)(2,1)S(1)} %fusion.3) | data formatting | bytes 327680 | tf_op jit(solution)/shard_map/convert_element_type | solution.py:442
  30.4 6.1 %copy.13 = bf16[8,8,8,2,5,16]{5,4,3,2,1,0:T(8,128)(2,1)S(1)} copy(bf16[8,8,8,2,5,16]{2,0,1,3,4,5:T(8,128)(2,1)} %bitcast.18) | data formatting | bytes 327680 | tf_op jit(solution)/shard_map/convert_element_type | solution.py:442
  36.5 2.3 %reshape.258.lat_ref = bf16[8,64,160]{2,1,0:T(8,128)(2,1)} reshape(bf16[8,8,8,2,5,16]{5,4,3,2,1,0:T(8,128)(2,1)S(1)} %copy.13) | data formatting | bytes 327680 | tf_op jit(solution)/shard_map/reshape | solution.py:442
  38.8 17.8 %exchange.1 = (bf16[8,64,160]{2,1,0:T(8,128)(2,1)}, f32[16,3,8,128]{3,2,1,0:T(8,128)}) custom-call(bf16[8,64,160]{2,1,0:T(8,128)(2,1)} %reshape.258.lat_ref, f32[16,3,8,128]{3,2,1,0:T(8,128)} %normal_tables.1.norm_ref), custom_call_target="tpu_custom_call" | custom-call | tf_op jit(solution)/shard_map/exchange/pallas_call | solution.py:157
  56.6 0.0 copy-start.2
  56.6 0.9 copy-done.2
  57.6 0.9 copy-done.3
  58.5 5.8 %grid_stage.1.spec_ref = bf16[128,8,128]{2,1,0:T(8,128)(2,1)S(1)} custom-call(bf16[8,64,160]{2,1,0:T(8,128)(2,1)S(1)} %copy-done.2, f32[16,3,8,128]{3,2,1,0:T(8,128)S(1)} %copy-done.3, f32[4,640,128]{2,1,0:T(8,128)S(1)} %pad_maximum_fusion.trig_ref), custom_call_target="tpu_custom_call" | custom-call | tf_op jit(solution)/shard_map/grid_stage/pallas_call | solution.py:214
  64.3 0.0 copy-start.1
  64.4 0.7 copy-done.1
  65.1 31.8 %gram_stage.1 = (bf16[5,128,128]{2,1,0:T(8,128)(2,1)}, f32[8,16,128]{2,1,0:T(8,128)}) custom-call(bf16[128,8,128]{2,1,0:T(8,128)(2,1)} %copy-done.1, bf16[5,64,1200]{2,1,0:T(8,128)(2,1)} %constant_dynamic-slice_fusion.leg_ref), custom_call_target="tpu_custom_call" | custom-call | tf_op jit(solution)/shard_map/gram_stage/pallas_call | solution.py:319
  96.8 8.9 %panel_stage.1 = (f32[2,5,1200,128]{3,2,1,0:T(8,128)}, f32[128,128]{1,0:T(8,128)}) custom-call(f32[8,16,128]{2,1,0:T(8,128)} %get-tuple-element.10.gram_ref, bf16[5,128,128]{2,1,0:T(8,128)(2,1)} %get-tuple-element.11.rows_ref, bf16[5,64,1200]{2,1,0:T(8,128)(2,1)} %constant_dynamic-slice_fusion.leg_ref), custom_call_target="tpu_custom_call" | custom-call | tf_op jit(solution)/shard_map/panel_stage/pallas_call | solution.py:405
  (2 shorter events, 0.0 us)
Async XLA Ops:
  0.6 1.3 %copy-start = (s32[1,16,24]{2,1,0:T(8,128)S(1)}, s32[1,16,24]{2,1,0:T(8,128)}, u32[]{:S(2)}) copy-start(s32[1,16,24]{2,1,0:T(8,128)} %param.11) | copy-start | bytes 4612
  56.6 1.0 copy-start.2
  57.6 0.9 copy-start.3
  64.3 0.7 copy-start.1

commit v3 on v0

v3 whole, which is shorter than its diff:
```python
import math

import jax
import jax.numpy as jnp
from jax import lax
from jax.experimental import pallas as pl
from jax.experimental.pallas import tpu as pltpu
from jax.sharding import PartitionSpec as P

NDEG = 1200
ORDERS = 640
NLON = 1280
NC = 8
NT = 16
ND = NC * NT
OWN = 5
UNITS = 40
PIECE = 3
STEP = 8
CHUNKS = 10

BF = jnp.bfloat16
F32 = jnp.float32
HIGHEST = lax.Precision.HIGHEST
MESH = pl.DeviceIdType.MESH
VM = pl.BlockSpec(memory_space=pltpu.VMEM)


def mm(a, b):
    return lax.dot_general(a, b, (((1,), (0,)), ((), ())), preferred_element_type=F32)


def mm_nt(a, b):
    return lax.dot_general(a, b, (((1,), (1,)), ((), ())), preferred_element_type=F32)


def split(x):
    hi = x.astype(BF)
    return hi, (x - hi.astype(F32)).astype(BF)


def front_kernel(
    probes_ref, leg_ref, order_ref, index_ref, count_ref, base_ref, coef_ref, weight_ref,
    rows_out, gram_out,
    leg, prob, base, coef, weight, live, hist, norm, part, table, lat_rows, lat_pack, lat_send, lat_recv,
    cos_q, sin_q, cos_b, sin_b, tab_hi, tab_lo, adj_ref, spec_ref, turn_ref, spec, recv, perm, normal,
    g_part, g_coef, g_track, in_sem, leg_sem, prob_sem, comm,
):
    c = lax.axis_index("coef")
    t = lax.axis_index("track")
    me = c * NT + t

    def send(src, dst, k, pc, pt):
        pltpu.make_async_remote_copy(
            src, dst, comm.at[2 * k], comm.at[2 * k + 1], device_id=(pc, pt), device_id_type=MESH
        ).start()

    def arrived(ref, n, k):
        pltpu.make_async_copy(ref.at[pl.ds(0, n)], ref.at[pl.ds(0, n)], comm.at[2 * k + 1]).wait()

    def sent(ref, n, k):
        pltpu.make_async_copy(ref.at[pl.ds(0, n)], ref.at[pl.ds(0, n)], comm.at[2 * k]).wait()

    small = [
        pltpu.make_async_copy(src, dst, in_sem.at[k])
        for k, (src, dst) in enumerate(((base_ref, base), (coef_ref, coef), (weight_ref, weight)))
    ]
    for copy in small:
        copy.start()

    def fetch(k):
        orders = pl.ds(k * STEP, STEP)
        return (
            pltpu.make_async_copy(leg_ref.at[orders], leg.at[orders], leg_sem.at[k]),
            pltpu.make_async_copy(probes_ref.at[:, orders], prob.at[:, orders], prob_sem.at[k]),
        )

    for k in range(CHUNKS):
        for copy in fetch(k):
            copy.start()
    barrier = pltpu.get_barrier_semaphore()

    def greet(i, carry):
        peer = (me + i) % ND
        pl.semaphore_signal(barrier, 1, device_id=(peer // NT, peer % NT), device_id_type=MESH)
        return carry

    lax.fori_loop(1, ND, greet, 0)

    for copy in small:
        copy.wait()
    slots, obs = base.shape
    lane16 = lax.broadcasted_iota(jnp.int32, (1, NT), 1)
    count = jnp.sum(jnp.where(lane16 == t, count_ref[...].astype(F32), 0.0), axis=1, keepdims=True)
    slot_id = lax.broadcasted_iota(jnp.int32, (slots, obs), 0).astype(F32)
    live[...] = jnp.where(slot_id < count, weight[...], 0.0)
    points = lax.broadcasted_iota(jnp.int32, (128, obs), 0)

    def slot(group, carry):
        for u in range(4):
            s = group * 4 + u
            hot = jnp.where(points == base[pl.ds(s, 1), :], 1.0, 0.0).astype(BF)
            four = coef[s].astype(F32)
            eight = jnp.concatenate([four, jnp.zeros_like(four)], axis=0)
            scaled = eight * live[pl.ds(s, 1), :]
            full = jnp.concatenate(
                [scaled * eight] + [scaled * pltpu.roll(eight, 8 - d, axis=0) for d in range(1, 4)], axis=0
            )
            hi, mid = split(full)
            low = (full - hi.astype(F32) - mid.astype(F32)).astype(BF)
            sums = mm_nt(jnp.concatenate([hi, mid, low], axis=0), hot)
            hist[s] = sums[:32] + sums[32:64] + sums[64:]
        return carry

    lax.fori_loop(0, slots // 4, slot, 0)
    diagonals = []
    for d in range(4):
        total = hist[:, 8 * d, :]
        for i in range(1, 4 - d):
            total = total + pltpu.roll(hist[:, 8 * d + i, :], i, axis=1)
        diagonals.append(total)
    rows = lax.broadcasted_iota(jnp.int32, (80, slots), 0)
    tile = (rows & 7) * 10 + lax.shift_right_logical(rows, 3)
    pick = jnp.where(tile == index_ref[pl.ds(t, 1), :], 1.0, 0.0)
    summed = exact(pick, jnp.concatenate(diagonals, axis=1), NN)
    for u in range(NT * PIECE):
        if u < UNITS:
            b, d = u // 4, u % 4
            block = summed[b * 8 : (b + 1) * 8, d * 128 : (d + 1) * 128]
        else:
            block = jnp.zeros((8, 128), F32)
        norm[u // PIECE, u % PIECE] = block
    pl.semaphore_wait(barrier, ND - 1)
    for i in range(1, NT):
        peer = (t + i) % NT
        send(norm.at[peer], part.at[t], 0, c, peer)
    part[t] = norm[t]

    def lat_step(k, carry):
        for copy in fetch(k):
            copy.wait()
        for u in range(STEP):
            order = k * STEP + u
            both = mm_nt(prob[:, order].reshape(16, NDEG), leg[order])
            owner = order // OWN
            row = ((order - owner * OWN) * NT + owner) * 8
            lat_rows[pl.ds(pl.multiple_of(row, 8), 8), :] = jnp.concatenate([both[:8], both[8:]], axis=1)
        return carry

    lax.fori_loop(0, CHUNKS, lat_step, 0)
    for p in range(8):
        turned = lat_rows[pl.ds(p, 80, stride=8), :].T
        for half in range(2):
            for s in range(NC):
                start = half * 64 + s * 8
                lat_pack[s, half, p * 8 : (p + 1) * 8, :] = turned[start : start + 8, :]
    lat_send[...] = lat_pack[...].astype(BF)
    for i in range(1, NC):
        peer = (c + i) % NC
        send(lat_send.at[peer], lat_recv.at[c], 1, peer, t)
    lat_recv[c] = lat_send[c]
    arrived(part, NT - 1, 0)
    total = part[0]
    for s in range(1, NT):
        total = total + part[s]
    table[t] = total
    for i in range(1, NT):
        peer = (t + i) % NT
        send(table.at[t], table.at[t], 2, c, peer)

    orders = jnp.concatenate([order_ref[r : r + 1, :] for r in range(OWN)], axis=1)
    coarse = jnp.broadcast_to(lax.shift_right_logical(orders, 5).astype(F32).astype(BF), (128, ORDERS))
    fine = jnp.broadcast_to((orders & 31).astype(F32).astype(BF), (128, ORDERS))
    owner_row = lax.broadcasted_iota(jnp.int32, (128, ORDERS), 0) * OWN
    slot_lane = lax.broadcasted_iota(jnp.int32, (128, ORDERS), 1)
    lane = lax.broadcasted_iota(jnp.int32, (128, 128), 1).astype(F32)

    def trig(j, carry):
        hot = jnp.where(owner_row + j == slot_lane, 1.0, 0.0).astype(BF)
        order = 32.0 * mm_nt(hot, coarse) + mm_nt(hot, fine)
        cos_q[j], sin_q[j] = circle(order * lane)
        cosine, sine = circle(order * (lane * 128.0))
        cos_b[j] = cosine * (1.0 / math.sqrt(ORDERS))
        sin_b[j] = sine * (1.0 / math.sqrt(ORDERS))
        cq, sq, cb, sb = cos_q[j], sin_q[j], cos_b[j], sin_b[j]
        for b in range(10):
            ca, sa = cb[:, b : b + 1], sb[:, b : b + 1]
            cols = slice(b * 128, (b + 1) * 128)
            hi, lo = split(ca * cq - sa * sq)
            tab_hi[j, :, cols] = hi
            tab_lo[j, :, cols] = lo
            hi, lo = split(sa * cq + ca * sq)
            tab_hi[OWN + j, :, cols] = hi
            tab_lo[OWN + j, :, cols] = lo
        return carry

    lax.fori_loop(0, OWN, trig, 0)

    arrived(lat_recv, NC - 1, 1)
    grid = jnp.zeros((64, NLON), F32)
    for s in range(NC):
        own = slice(s * NT, (s + 1) * NT)
        for half in range(2):
            js = slice(half * OWN, (half + 1) * OWN)
            grid = grid + mm(lat_recv[s, half], tab_hi[js, own, :].reshape(80, NLON))
            grid = grid + mm(lat_recv[s, half], tab_lo[js, own, :].reshape(80, NLON))
    arrived(table, NT - 1, 2)
    for b in range(10):
        x = grid[:, b * 128 : (b + 1) * 128]

        def diagonal(d):
            unit = b * 4 + d
            block = table[unit // PIECE, unit % PIECE]
            return jnp.broadcast_to(block[None], (8, 8, 128)).reshape(64, 128)

        adj = diagonal(0) * x
        for d in range(1, 4):
            m = diagonal(d)
            adj = adj + m * pltpu.roll(x, 128 - d, axis=1) + pltpu.roll(m * x, d, axis=1)
        hi, lo = split(adj)
        adj_ref[:64, b * 128 : (b + 1) * 128] = hi
        adj_ref[64:, b * 128 : (b + 1) * 128] = lo
    for i in range(10):
        both = mm_nt(adj_ref[...], tab_hi[i])
        spec_ref[i] = both[:64] + both[64:] + mm_nt(adj_ref[:64, :], tab_lo[i])
    spec_ref[10:] = jnp.zeros((6, 64, 128), F32)
    for p in range(8):
        block = spec_ref[:, p * 8 : (p + 1) * 8, :].reshape(128, 128)
        turn_ref[pl.ds(p, 128, stride=8), :] = block.T
    spec[...] = turn_ref[...].reshape(128, 8, 128).astype(BF)

    def scatter(i, carry):
        peer = (me + i) % ND
        send(spec.at[peer], recv.at[me], 3, peer // NT, peer % NT)
        return carry

    lax.fori_loop(1, ND, scatter, 0)
    recv[me] = spec[me]

    same = (lax.broadcasted_iota(jnp.int32, (128, 128), 0) < 64) == (
        lax.broadcasted_iota(jnp.int32, (128, 128), 1) < 64
    )
    for j in range(OWN):
        one = leg[t * OWN + j]
        two = jnp.concatenate([one, one], axis=0)
        hi, lo = split(jnp.where(same, mm_nt(two, two), 0.0))
        normal[0, j] = hi
        normal[1, j] = lo
    row = lax.broadcasted_iota(jnp.int32, (128, 640), 0)
    col = lax.broadcasted_iota(jnp.int32, (128, 640), 1)
    src_i, src_a = lax.shift_right_logical(row, 3), row & 7
    dst_i = (lax.shift_right_logical(col, 6) & 1) * OWN + lax.shift_right_logical(col, 7)
    dst_band, dst_a = lax.shift_right_logical(col, 3) & 7, col & 7
    hit = (src_a == dst_a) & (src_i == dst_i)
    for s in range(NC):
        perm[s * 128 : (s + 1) * 128, :] = jnp.where(hit & (dst_band == s), 1.0, 0.0).astype(BF)
    arrived(recv, ND - 1, 3)
    gathered = jnp.zeros((128, 640), F32)
    for s in range(NC):
        block = recv[s * NT : (s + 1) * NT].astype(F32).reshape(128, 128).astype(BF)
        gathered = gathered + mm(block, perm[s * 128 : (s + 1) * 128, :])
    gram = jnp.zeros((128, 128), F32)
    for j in range(OWN):
        mine = gathered[:, j * 128 : (j + 1) * 128].astype(BF)
        rows_out[j] = mine
        hi, lo = split(mm(mine, normal[0, j]) + mm(mine, normal[1, j]))
        gram = gram + mm_nt(hi, mine) + mm_nt(lo, mine)
    g_part[...] = gram.reshape(NC, 16, 128)
    for i in range(1, NC):
        peer = (c + i) % NC
        send(g_part.at[peer], g_coef.at[c], 4, peer, t)
    g_coef[c] = g_part[c]
    arrived(g_coef, NC - 1, 4)
    total = g_coef[0]
    for s in range(1, NC):
        total = total + g_coef[s]
    g_track[t] = total
    for i in range(1, NT):
        peer = (t + i) % NT
        send(g_track.at[t], g_track.at[t], 5, c, peer)
    arrived(g_track, NT - 1, 5)
    total = g_track[0]
    for s in range(1, NT):
        total = total + g_track[s]
    gram_out[c] = total * (1.0 / (2 * ORDERS * NDEG))
    for i in range(1, NC):
        peer = (c + i) % NC
        send(gram_out.at[c], gram_out.at[c], 6, peer, t)
    arrived(gram_out, NC - 1, 6)
    for ref, n, k in (
        (part, NT - 1, 0), (lat_send, NC - 1, 1), (table, NT - 1, 2), (spec, ND - 1, 3),
        (g_part, NC - 1, 4), (g_track, NT - 1, 5), (gram_out, NC - 1, 6),
    ):
        sent(ref, n, k)


def circle(x):
    quarter = jnp.floor(x * (1.0 / 320.0) + 0.5)
    y = (x - quarter * 320.0) * (2.0 * math.pi / NLON)
    turn = quarter - 4.0 * jnp.floor(quarter * 0.25)
    z = y * y
    sine = y * (1.0 + z * (-1.0 / 6 + z * (1.0 / 120 + z * (-1.0 / 5040 + z * (1.0 / 362880)))))
    cosine = 1.0 + z * (-0.5 + z * (1.0 / 24 + z * (-1.0 / 720 + z * (1.0 / 40320 - z * (1.0 / 3628800)))))
    odd = (turn == 1.0) | (turn == 3.0)
    cos_x = jnp.where(odd, sine, cosine)
    sin_x = jnp.where(odd, cosine, sine)
    cos_x = jnp.where((turn == 1.0) | (turn == 2.0), -cos_x, cos_x)
    sin_x = jnp.where(turn >= 2.0, -sin_x, sin_x)
    return cos_x, sin_x


def front_stage(probes, legendre, orders, index, count, base, coef, weight):
    slots, obs = base.shape
    vm = pltpu.VMEM
    any_space = pl.BlockSpec(memory_space=pl.ANY)
    return pl.pallas_call(
        front_kernel,
        name="front_stage",
        out_shape=(jax.ShapeDtypeStruct((OWN, 128, 128), BF), jax.ShapeDtypeStruct((NC, 16, 128), F32)),
        in_specs=[any_space, any_space, VM, VM, VM, any_space, any_space, any_space],
        out_specs=(VM, VM),
        scratch_shapes=[
            vm(legendre.shape, BF), vm(probes.shape, BF),
            vm(base.shape, jnp.int32), vm(coef.shape, BF), vm(weight.shape, F32), vm(weight.shape, F32),
            vm((slots, 32, 128), F32),
            vm((NT, PIECE, 8, 128), F32), vm((NT, PIECE, 8, 128), F32), vm((NT, PIECE, 8, 128), F32),
            vm((640, 128), F32),
            vm((NC, 2, 64, 80), F32), vm((NC, 2, 64, 80), BF), vm((NC, 2, 64, 80), BF),
            vm((OWN, 128, 128), F32), vm((OWN, 128, 128), F32), vm((OWN, 128, 128), F32), vm((OWN, 128, 128), F32),
            vm((10, 128, NLON), BF), vm((10, 128, NLON), BF),
            vm((128, NLON), BF), vm((16, 64, 128), F32), vm((1024, 128), F32),
            vm((ND, 8, 128), BF), vm((ND, 8, 128), BF), vm((1024, 640), BF), vm((2, OWN, 128, 128), BF),
            vm((NC, 16, 128), F32), vm((NC, 16, 128), F32), vm((NT, 16, 128), F32),
            pltpu.SemaphoreType.DMA((3,)), pltpu.SemaphoreType.DMA((CHUNKS,)),
            pltpu.SemaphoreType.DMA((CHUNKS,)), pltpu.SemaphoreType.DMA((14,)),
        ],
        compiler_params=pltpu.CompilerParams(
            collective_id=0, has_side_effects=True, vmem_limit_bytes=56 * 1024 * 1024
        ),
    )(probes, legendre, orders, index, count, base, coef, weight)


def exact(a, b, dims):
    return lax.dot_general(a, b, (dims, ((), ())), precision=HIGHEST, preferred_element_type=F32)


NN = ((1,), (0,))
NT_DIMS = ((1,), (1,))


def factorize(gram, upper_ref, inv_ref):
    n = gram.shape[0]
    row = lax.broadcasted_iota(jnp.int32, (n, n), 0)
    col = lax.broadcasted_iota(jnp.int32, (n, n), 1)
    eye = jnp.where(row == col, 1.0, 0.0)
    half = jnp.where(row > col, 1.0, 0.5 * eye)
    diag = jnp.where(row == col, gram, 0.0)
    r_col = lax.rsqrt(jnp.sum(diag, axis=1, keepdims=True))
    r_row = lax.rsqrt(jnp.sum(diag, axis=0, keepdims=True))
    inverse = (eye - half * (gram * r_col * r_row - eye)) * r_row
    error = eye
    for _ in range(3):
        error = exact(exact(inverse, gram, NN), inverse, NT_DIMS) - eye
        inverse = inverse - exact(half * error, inverse, NN)
    inv_ref[...] = inverse
    upper_ref[...] = jnp.where(row <= col, exact(inverse, gram, NN), 0.0)
    worst = jnp.max(jnp.abs(error))

    @pl.when(jnp.logical_not(worst < 1e-4))
    def _():
        def column(j, state):
            left, upper, inv = state
            at_row, at_col = row == j, col == j
            line = jnp.sum(jnp.where(at_row, left, 0.0), axis=0, keepdims=True)
            down = jnp.sum(jnp.where(at_col, left, 0.0), axis=1, keepdims=True)
            pivot = jnp.sum(jnp.where(at_row & at_col, left, 0.0), keepdims=True)
            scale = 1.0 / jnp.sqrt(pivot)
            line = jnp.where(col[:1] >= j, line * scale, 0.0)
            below = jnp.where(row[:, :1] > j, down * scale, 0.0)
            inv_line = jnp.sum(jnp.where(at_row, inv, 0.0), axis=0, keepdims=True) * scale
            inv = jnp.where(at_row, inv_line, inv - below * inv_line)
            upper = jnp.where(at_row, line, upper)
            return left - below * line, upper, inv

        _, upper, inv = lax.fori_loop(0, n, column, (gram, jnp.zeros_like(gram), eye))
        upper_ref[...] = upper
        inv_ref[...] = inv


def panel_kernel(first_ref, gram_ref, rows_ref, leg_ref, out_ref, upper_ref, inv_ref):
    @pl.when(pl.program_id(0) == 0)
    def _():
        factorize(gram_ref[...].reshape(128, 128), upper_ref, inv_ref)

    hi, lo = split(inv_ref[...])
    z = mm(hi, rows_ref[0]) + mm(lo, rows_ref[0])
    z_hi, z_lo = split(z)
    left = lax.broadcasted_iota(jnp.int32, (128, 128), 1) < 64
    hi_f, lo_f = z_hi.astype(F32), z_lo.astype(F32)
    cosine = jnp.where(left, hi_f, pltpu.roll(lo_f, 64, axis=1)).astype(BF)
    sine = jnp.where(left, pltpu.roll(hi_f, 64, axis=1), lo_f).astype(BF)
    one = leg_ref[0]
    two = jnp.concatenate([one, one], axis=0)
    contract = (((0,), (1,)), ((), ()))
    out_ref[0, 0] = lax.dot_general(two, cosine, contract, preferred_element_type=F32)
    out_ref[1, 0] = lax.dot_general(two, sine, contract, preferred_element_type=F32)


def panel_stage(first, gram, rows, legendre):
    return pl.pallas_call(
        panel_kernel,
        name="panel_stage",
        out_shape=(
            jax.ShapeDtypeStruct((2, OWN, NDEG, 128), F32),
            jax.ShapeDtypeStruct((128, 128), F32),
        ),
        grid_spec=pltpu.PrefetchScalarGridSpec(
            num_scalar_prefetch=1,
            grid=(OWN,),
            in_specs=[
                pl.BlockSpec((NC, 16, 128), lambda j, first: (0, 0, 0)),
                pl.BlockSpec((1, 128, 128), lambda j, first: (j, 0, 0)),
                pl.BlockSpec((1, 64, NDEG), lambda j, first: (first[0] + j, 0, 0)),
            ],
            out_specs=(
                pl.BlockSpec((2, 1, NDEG, 128), lambda j, first: (0, j, 0, 0)),
                pl.BlockSpec((128, 128), lambda j, first: (0, 0)),
            ),
            scratch_shapes=[pltpu.VMEM((128, 128), F32)],
        ),
    )(first, gram, rows, legendre)


def on_device(
    probes, legendre, order_map, tile_index, tile_count, base_offset, stencil_weight, obs_weight
):
    rows, gram = front_stage(
        probes, legendre, order_map.reshape(OWN, 128), tile_index[0], tile_count,
        base_offset[0, 0], stencil_weight[0, 0], obs_weight[0, 0],
    )
    first = jnp.reshape(lax.axis_index("track") * OWN, (1,))
    panel, upper = panel_stage(first, gram, rows, legendre)
    return (jnp.swapaxes(panel, 2, 3), upper)


def solution(mesh):
    return jax.shard_map(
        on_device,
        mesh=mesh,
        in_specs=(
            P(None, "coef", "track", None),
            P("coef", None, None),
            P(),
            P("coef", None, None),
            P("coef", None),
            P("coef", "track", None, None),
            P("coef", "track", None, None, None),
            P("coef", "track", None, None),
        ),
        out_specs=(P(None, ("coef", "track"), None, None), P()),
        check_vma=False,
    )
```

time: 417 us -> 60.5 us (0.15); the launches traced: 409 us -> 60.3 us
  waiting for transfers between devices: 185 us -> 0 us
  matrix products: 84.7 us -> 0 us
  Pallas kernels: 0 us -> 59.6 us
  other arithmetic: 45.6 us -> 0 us
  local copies, waits for them, and re-layouts: 44.2 us -> 0 us
  starting transfers between devices: 18.4 us -> 0 us
  blocking collectives: 16.9 us -> 0 us
  between operations: 14.7 us -> 0.64 us
    psum x1 -> x0, waiting for transfers between devices: 137 us -> none  [on_device(): gram = lax.psum(gram_part, ('coef', 'track')) / (2 * ORDERS * NDEG)]
    dot_general x9 -> x0, matrix products: 84.5 us -> none  [the longest x1 19.9 us: on_device(): jnp.einsum('soq,sop->spq', stencil, resid, preferred_element_type=jnp.flo...]
    pallas_call x0 -> x2, Pallas kernels: none -> 59.6 us  [the longest x1 50.7 us: front_stage(): pl.pallas_call(front_kernel, name='front_stage', out_shape=(jax.ShapeDtyp...]
    reduce_scatter x1 -> x0, waiting for transfers between devices: 33.8 us -> none  [on_device(): lax.psum_scatter(jnp.einsum('cmpa,cmbq->abpq', lat_coef, local_tables, pr...]
    unnamed x29 -> x0, local copies, waits for them, and re-layouts: 26.8 us -> none
    another operation x4 -> x0, other arithmetic: 22.4 us -> none  [the longest x3 12.6 us: on_device(): lower = jnp.linalg.cholesky(gram)]
    all_to_all x3 -> x0, starting transfers between devices: 18.1 us -> none  [the longest x1 6.97 us: on_device(): lax.all_to_all(rounded, 'track', split_axis=1, concat_axis=2, tiled=True)]
    all_to_all x1 -> x0, blocking collectives: 16.9 us -> none  [on_device(): lax.all_to_all(spectra.astype(jnp.bfloat16), 'coef', split_axis=1, concat...]
  transfers between devices with their start and end apart: 5 -> 0, of which waited for: 4 -> 0; matrix products, arithmetic and copies ran while one was open for 5% -> 0% of each run, Pallas kernels for 0% -> 0%
where the time goes in v3:
time: 60.5 us; the launch traced here: 60.3 us
  Pallas kernels  59.6 us (99%)
  between operations  0.64 us (1%)
    pallas_call x1, Pallas kernels, front_stage(): pl.pallas_call(front_kernel, name='front_stage', out_shape=(jax.ShapeDtyp...  50.7 us
    pallas_call x1, Pallas kernels, panel_stage(): pl.pallas_call(panel_kernel, name='panel_stage', out_shape=(jax.ShapeDtyp...  8.9 us

profile of v3, /device:TPU:1, one launch (start us, length us, event | category | flops | bytes accessed | tf_op | source)
XLA Modules:
  0.0 60.3 jit_solution(247753651564140338)
XLA Ops:
  0.6 50.7 %front_stage.1 = (bf16[5,128,128]{2,1,0:T(8,128)(2,1)}, f32[8,16,128]{2,1,0:T(8,128)}) custom-call(bf16[2,80,8,1200]{3,2,1,0:T(8,128)(2,1)} %probes_ref.1, bf16[80,64,1200]{2,1,0:T(8,128)(2,1)} %leg_ref.3, s32[5,128]{1,0:T(8,128)} %bitcast.11, s32[16,24]{1,0:T(8,128)} %bitcast.10, s32[1,16]{1,0:T(1,128)} %count_ref.1, s32[24,512]{1,0:T(8,128)} %bitcast.8, ...), custom_call_target="tpu_custom_call" | custom-call | tf_op jit(solution)/shard_map/front_stage/pallas_call | solution.py:316
  51.4 8.9 %panel_stage.1 = (f32[2,5,1200,128]{3,2,1,0:T(8,128)}, f32[128,128]{1,0:T(8,128)}) custom-call(s32[1]{0:T(128)} %bitcast.first_ref, f32[8,16,128]{2,1,0:T(8,128)} %get-tuple-element.6.gram_ref, bf16[5,128,128]{2,1,0:T(8,128)(2,1)} %get-tuple-element.7.rows_ref, bf16[80,64,1200]{2,1,0:T(8,128)(2,1)} %leg_ref.3), custom_call_target="tpu_custom_call" | custom-call | tf_op jit(solution)/shard_map/panel_stage/pallas_call | solution.py:410

commit v4 on v3

--- a/solution.py
+++ b/solution.py
@@ -16,8 +16,8 @@
 OWN = 5
 UNITS = 40
 PIECE = 3
-STEP = 8
-CHUNKS = 10
+STEP = 16
+CHUNKS = 5
 
 BF = jnp.bfloat16
 F32 = jnp.float32
@@ -41,10 +41,10 @@
 
 def front_kernel(
     probes_ref, leg_ref, order_ref, index_ref, count_ref, base_ref, coef_ref, weight_ref,
-    rows_out, gram_out,
+    rows_out, gram_out, turned_out,
     leg, prob, base, coef, weight, live, hist, norm, part, table, lat_rows, lat_pack, lat_send, lat_recv,
     cos_q, sin_q, cos_b, sin_b, tab_hi, tab_lo, adj_ref, spec_ref, turn_ref, spec, recv, perm, normal,
-    g_part, g_coef, g_track, in_sem, leg_sem, prob_sem, comm,
+    g_part, g_coef, g_track, turned_leg, in_sem, leg_sem, prob_sem, turn_sem, comm, ready,
 ):
     c = lax.axis_index("coef")
     t = lax.axis_index("track")
@@ -60,6 +60,15 @@
 
     def sent(ref, n, k):
         pltpu.make_async_copy(ref.at[pl.ds(0, n)], ref.at[pl.ds(0, n)], comm.at[2 * k]).wait()
+
+    z, core = lax.div(c, 2), lax.rem(c, 2)
+    y, x = lax.div(t, 4), lax.rem(t, 4)
+    far = (0, 1, 2, 1)
+    bands = {(dz, dk): lax.rem(z + dz, 4) * 2 + lax.rem(core + dk, 2) for dz in range(4) for dk in range(2)}
+    tracks = {(dy, dx): lax.rem(y + dy, 4) * 4 + lax.rem(x + dx, 4) for dy in range(4) for dx in range(4)}
+    steps = [(dz, dk, dy, dx) for dz in range(4) for dk in range(2) for dy in range(4) for dx in range(4)]
+    steps.sort(key=lambda d: -(far[d[0]] + far[d[2]] + far[d[3]]) * 2 - d[1])
+    peers = [(bands[d[:2]], tracks[d[2:]]) for d in steps if any(d)]
 
     small = [
         pltpu.make_async_copy(src, dst, in_sem.at[k])
@@ -75,20 +84,18 @@
             pltpu.make_async_copy(probes_ref.at[:, orders], prob.at[:, orders], prob_sem.at[k]),
         )
 
+    barrier = pltpu.get_barrier_semaphore()
+
+    for i in range(1, NC):
+        pl.semaphore_signal(barrier, 1, device_id=(lax.rem(c + i, NC), t), device_id_type=MESH)
+    for i in range(1, NT):
+        pl.semaphore_signal(barrier, 1, device_id=(c, lax.rem(t + i, NT)), device_id_type=MESH)
+
+    for copy in small:
+        copy.wait()
     for k in range(CHUNKS):
         for copy in fetch(k):
             copy.start()
-    barrier = pltpu.get_barrier_semaphore()
-
-    def greet(i, carry):
-        peer = (me + i) % ND
-        pl.semaphore_signal(barrier, 1, device_id=(peer // NT, peer % NT), device_id_type=MESH)
-        return carry
-
-    lax.fori_loop(1, ND, greet, 0)
-
-    for copy in small:
-        copy.wait()
     slots, obs = base.shape
     lane16 = lax.broadcasted_iota(jnp.int32, (1, NT), 1)
     count = jnp.sum(jnp.where(lane16 == t, count_ref[...].astype(F32), 0.0), axis=1, keepdims=True)
@@ -130,7 +137,9 @@
         else:
             block = jnp.zeros((8, 128), F32)
         norm[u // PIECE, u % PIECE] = block
-    pl.semaphore_wait(barrier, ND - 1)
+    pl.semaphore_wait(barrier, NC + NT - 2)
+    for i in range(1, NT):
+        pl.semaphore_signal(ready, 1, device_id=(c, lax.rem(t + i, NT)), device_id_type=MESH)
     for i in range(1, NT):
         peer = (t + i) % NT
         send(norm.at[peer], part.at[t], 0, c, peer)
@@ -229,12 +238,9 @@
         turn_ref[pl.ds(p, 128, stride=8), :] = block.T
     spec[...] = turn_ref[...].reshape(128, 8, 128).astype(BF)
 
-    def scatter(i, carry):
-        peer = (me + i) % ND
-        send(spec.at[peer], recv.at[me], 3, peer // NT, peer % NT)
-        return carry
-
-    lax.fori_loop(1, ND, scatter, 0)
+    pl.semaphore_wait(ready, NT - 1)
+    for pc, pt in peers:
+        send(spec.at[pc * NT + pt], recv.at[me], 3, pc, pt)
     recv[me] = spec[me]
 
     same = (lax.broadcasted_iota(jnp.int32, (128, 128), 0) < 64) == (
@@ -266,10 +272,18 @@
         hi, lo = split(mm(mine, normal[0, j]) + mm(mine, normal[1, j]))
         gram = gram + mm_nt(hi, mine) + mm_nt(lo, mine)
     g_part[...] = gram.reshape(NC, 16, 128)
+
+    def turn(j):
+        one = leg[t * OWN + j]
+        turned_leg[j] = jnp.concatenate([one, one], axis=0).T
+        pltpu.make_async_copy(turned_leg.at[j], turned_out.at[j], turn_sem.at[j]).start()
+
     for i in range(1, NC):
         peer = (c + i) % NC
         send(g_part.at[peer], g_coef.at[c], 4, peer, t)
     g_coef[c] = g_part[c]
+    turn(0)
+    turn(1)
     arrived(g_coef, NC - 1, 4)
     total = g_coef[0]
     for s in range(1, NC):
@@ -278,6 +292,8 @@
     for i in range(1, NT):
         peer = (t + i) % NT
         send(g_track.at[t], g_track.at[t], 5, c, peer)
+    turn(2)
+    turn(3)
     arrived(g_track, NT - 1, 5)
     total = g_track[0]
     for s in range(1, NT):
@@ -286,7 +302,10 @@
     for i in range(1, NC):
         peer = (c + i) % NC
         send(gram_out.at[c], gram_out.at[c], 6, peer, t)
+    turn(4)
     arrived(gram_out, NC - 1, 6)
+    for j in range(OWN):
+        pltpu.make_async_copy(turned_leg.at[j], turned_out.at[j], turn_sem.at[j]).wait()
     for ref, n, k in (
         (part, NT - 1, 0), (lat_send, NC - 1, 1), (table, NT - 1, 2), (spec, ND - 1, 3),
         (g_part, NC - 1, 4), (g_track, NT - 1, 5), (gram_out, NC - 1, 6),
@@ -316,9 +335,10 @@
     return pl.pallas_call(
         front_kernel,
         name="front_stage",
-        out_shape=(jax.ShapeDtypeStruct((OWN, 128, 128), BF), jax.ShapeDtypeStruct((NC, 16, 128), F32)),
+        out_shape=(jax.ShapeDtypeStruct((OWN, 128, 128), BF), jax.ShapeDtypeStruct((NC, 16, 128), F32),
+                   jax.ShapeDtypeStruct((OWN, NDEG, 128), BF)),
         in_specs=[any_space, any_space, VM, VM, VM, any_space, any_space, any_space],
-        out_specs=(VM, VM),
+        out_specs=(VM, VM, any_space),
         scratch_shapes=[
             vm(legendre.shape, BF), vm(probes.shape, BF),
             vm(base.shape, jnp.int32), vm(coef.shape, BF), vm(weight.shape, F32), vm(weight.shape, F32),
@@ -331,8 +351,10 @@
             vm((128, NLON), BF), vm((16, 64, 128), F32), vm((1024, 128), F32),
             vm((ND, 8, 128), BF), vm((ND, 8, 128), BF), vm((1024, 640), BF), vm((2, OWN, 128, 128), BF),
             vm((NC, 16, 128), F32), vm((NC, 16, 128), F32), vm((NT, 16, 128), F32),
+            vm((OWN, NDEG, 128), BF),
             pltpu.SemaphoreType.DMA((3,)), pltpu.SemaphoreType.DMA((CHUNKS,)),
-            pltpu.SemaphoreType.DMA((CHUNKS,)), pltpu.SemaphoreType.DMA((14,)),
+            pltpu.SemaphoreType.DMA((CHUNKS,)), pltpu.SemaphoreType.DMA((OWN,)), pltpu.SemaphoreType.DMA((14,)),
+            pltpu.SemaphoreType.REGULAR,
         ],
         compiler_params=pltpu.CompilerParams(
             collective_id=0, has_side_effects=True, vmem_limit_bytes=56 * 1024 * 1024
@@ -345,7 +367,12 @@
 
 
 NN = ((1,), (0,))
-NT_DIMS = ((1,), (1,))
+
+
+def three(a, b, product):
+    a_hi, a_lo = split(a)
+    b_hi, b_lo = split(b)
+    return product(a_hi, b_hi) + product(a_hi, b_lo) + product(a_lo, b_hi)
 
 
 def factorize(gram, upper_ref, inv_ref):
@@ -360,10 +387,10 @@
     inverse = (eye - half * (gram * r_col * r_row - eye)) * r_row
     error = eye
     for _ in range(3):
-        error = exact(exact(inverse, gram, NN), inverse, NT_DIMS) - eye
-        inverse = inverse - exact(half * error, inverse, NN)
+        error = three(three(inverse, gram, mm), inverse, mm_nt) - eye
+        inverse = inverse - three(half * error, inverse, mm)
     inv_ref[...] = inverse
-    upper_ref[...] = jnp.where(row <= col, exact(inverse, gram, NN), 0.0)
+    upper_ref[...] = jnp.where(row <= col, three(inverse, gram, mm), 0.0)
     worst = jnp.max(jnp.abs(error))
 
     @pl.when(jnp.logical_not(worst < 1e-4))
@@ -387,7 +414,7 @@
         inv_ref[...] = inv
 
 
-def panel_kernel(first_ref, gram_ref, rows_ref, leg_ref, out_ref, upper_ref, inv_ref):
+def panel_kernel(gram_ref, rows_ref, leg_ref, out_ref, upper_ref, inv_ref):
     @pl.when(pl.program_id(0) == 0)
     def _():
         factorize(gram_ref[...].reshape(128, 128), upper_ref, inv_ref)
@@ -399,47 +426,40 @@
     hi_f, lo_f = z_hi.astype(F32), z_lo.astype(F32)
     cosine = jnp.where(left, hi_f, pltpu.roll(lo_f, 64, axis=1)).astype(BF)
     sine = jnp.where(left, pltpu.roll(hi_f, 64, axis=1), lo_f).astype(BF)
-    one = leg_ref[0]
-    two = jnp.concatenate([one, one], axis=0)
-    contract = (((0,), (1,)), ((), ()))
-    out_ref[0, 0] = lax.dot_general(two, cosine, contract, preferred_element_type=F32)
-    out_ref[1, 0] = lax.dot_general(two, sine, contract, preferred_element_type=F32)
-
-
-def panel_stage(first, gram, rows, legendre):
+    out_ref[0, 0] = mm_nt(leg_ref[0], cosine)
+    out_ref[1, 0] = mm_nt(leg_ref[0], sine)
+
+
+def panel_stage(gram, rows, turned):
     return pl.pallas_call(
         panel_kernel,
         name="panel_stage",
+        grid=(OWN,),
         out_shape=(
             jax.ShapeDtypeStruct((2, OWN, NDEG, 128), F32),
             jax.ShapeDtypeStruct((128, 128), F32),
         ),
-        grid_spec=pltpu.PrefetchScalarGridSpec(
-            num_scalar_prefetch=1,
-            grid=(OWN,),
-            in_specs=[
-                pl.BlockSpec((NC, 16, 128), lambda j, first: (0, 0, 0)),
-                pl.BlockSpec((1, 128, 128), lambda j, first: (j, 0, 0)),
-                pl.BlockSpec((1, 64, NDEG), lambda j, first: (first[0] + j, 0, 0)),
-            ],
-            out_specs=(
-                pl.BlockSpec((2, 1, NDEG, 128), lambda j, first: (0, j, 0, 0)),
-                pl.BlockSpec((128, 128), lambda j, first: (0, 0)),
-            ),
-            scratch_shapes=[pltpu.VMEM((128, 128), F32)],
+        in_specs=[
+            pl.BlockSpec((NC, 16, 128), lambda j: (0, 0, 0)),
+            pl.BlockSpec((1, 128, 128), lambda j: (j, 0, 0)),
+            pl.BlockSpec((1, NDEG, 128), lambda j: (j, 0, 0)),
+        ],
+        out_specs=(
+            pl.BlockSpec((2, 1, NDEG, 128), lambda j: (0, j, 0, 0)),
+            pl.BlockSpec((128, 128), lambda j: (0, 0)),
         ),
-    )(first, gram, rows, legendre)
+        scratch_shapes=[pltpu.VMEM((128, 128), F32)],
+    )(gram, rows, turned)
 
 
 def on_device(
     probes, legendre, order_map, tile_index, tile_count, base_offset, stencil_weight, obs_weight
 ):
-    rows, gram = front_stage(
+    rows, gram, turned = front_stage(
         probes, legendre, order_map.reshape(OWN, 128), tile_index[0], tile_count,
         base_offset[0, 0], stencil_weight[0, 0], obs_weight[0, 0],
     )
-    first = jnp.reshape(lax.axis_index("track") * OWN, (1,))
-    panel, upper = panel_stage(first, gram, rows, legendre)
+    panel, upper = panel_stage(gram, rows, turned)
     return (jnp.swapaxes(panel, 2, 3), upper)
 
 

time: 60.5 us -> 54.7 us (0.904)
  Pallas kernels: 59.6 us -> 53.7 us
    pallas_call x1, Pallas kernels: 50.7 us -> 45.3 us  [front_stage(): pl.pallas_call(front_kernel, name='front_stage', out_shape=(jax.ShapeDtyp...]
where the time goes in v4:
time: 54.7 us; the launch traced here: 54.4 us
  Pallas kernels  53.7 us (98%)
  between operations  0.64 us (1%)
    pallas_call x1, Pallas kernels, front_stage(): pl.pallas_call(front_kernel, name='front_stage', out_shape=(jax.ShapeDtyp...  45.3 us
    pallas_call x1, Pallas kernels, panel_stage(): pl.pallas_call(panel_kernel, name='panel_stage', grid=(OWN,), out_shape=(...  8.46 us

profile of v4, /device:TPU:1, one launch (start us, length us, event | category | flops | bytes accessed | tf_op | source)
XLA Modules:
  0.0 54.4 jit_solution(10112201277871509089)
XLA Ops:
  0.6 45.3 %front_stage.1 = (bf16[5,128,128]{2,1,0:T(8,128)(2,1)}, f32[8,16,128]{2,1,0:T(8,128)}, bf16[5,1200,128]{2,1,0:T(8,128)(2,1)}) custom-call(bf16[2,80,8,1200]{3,2,1,0:T(8,128)(2,1)} %probes_ref.1, bf16[80,64,1200]{2,1,0:T(8,128)(2,1)} %leg_ref.1, s32[5,128]{1,0:T(8,128)} %bitcast.10, s32[16,24]{1,0:T(8,128)} %bitcast.9, s32[1,16]{1,0:T(1,128)} %count_ref.1, ...), custom_call_target="tpu_custom_call" | custom-call | tf_op jit(solution)/shard_map/front_stage/pallas_call | solution.py:335
  45.9 8.5 %panel_stage.1 = (f32[2,5,1200,128]{3,2,1,0:T(8,128)}, f32[128,128]{1,0:T(8,128)}) custom-call(f32[8,16,128]{2,1,0:T(8,128)} %get-tuple-element.7.gram_ref, bf16[5,128,128]{2,1,0:T(8,128)(2,1)} %get-tuple-element.8.rows_ref, bf16[5,1200,128]{2,1,0:T(8,128)(2,1)} %get-tuple-element.9.leg_ref), custom_call_target="tpu_custom_call" | custom-call | tf_op jit(solution)/shard_map/panel_stage/pallas_call | solution.py:434

commit v5 on v4

--- a/solution.py
+++ b/solution.py
@@ -16,8 +16,8 @@
 OWN = 5
 UNITS = 40
 PIECE = 3
-STEP = 16
-CHUNKS = 5
+STEP = 20
+CHUNKS = 4
 
 BF = jnp.bfloat16
 F32 = jnp.float32
@@ -385,18 +385,21 @@
     r_col = lax.rsqrt(jnp.sum(diag, axis=1, keepdims=True))
     r_row = lax.rsqrt(jnp.sum(diag, axis=0, keepdims=True))
     inverse = (eye - half * (gram * r_col * r_row - eye)) * r_row
+    upper = three(inverse, gram, mm)
     error = eye
     for _ in range(3):
-        error = three(three(inverse, gram, mm), inverse, mm_nt) - eye
-        inverse = inverse - three(half * error, inverse, mm)
+        error = three(upper, inverse, mm_nt) - eye
+        step = three(half * error, jnp.concatenate([inverse, upper], axis=1), mm)
+        inverse = inverse - step[:, :n]
+        upper = upper - step[:, n:]
     inv_ref[...] = inverse
-    upper_ref[...] = jnp.where(row <= col, three(inverse, gram, mm), 0.0)
-    worst = jnp.max(jnp.abs(error))
-
-    @pl.when(jnp.logical_not(worst < 1e-4))
+    upper_ref[...] = jnp.where(row <= col, upper, 0.0)
+    failed = jnp.max(jnp.where(jnp.abs(error) < 1e-4, 0.0, 1.0))
+
+    @pl.when(failed > 0.5)
     def _():
         def column(j, state):
-            left, upper, inv = state
+            left, full, inv = state
             at_row, at_col = row == j, col == j
             line = jnp.sum(jnp.where(at_row, left, 0.0), axis=0, keepdims=True)
             down = jnp.sum(jnp.where(at_col, left, 0.0), axis=1, keepdims=True)
@@ -406,49 +409,67 @@
             below = jnp.where(row[:, :1] > j, down * scale, 0.0)
             inv_line = jnp.sum(jnp.where(at_row, inv, 0.0), axis=0, keepdims=True) * scale
             inv = jnp.where(at_row, inv_line, inv - below * inv_line)
-            upper = jnp.where(at_row, line, upper)
-            return left - below * line, upper, inv
-
-        _, upper, inv = lax.fori_loop(0, n, column, (gram, jnp.zeros_like(gram), eye))
-        upper_ref[...] = upper
+            return left - below * line, jnp.where(at_row, line, full), inv
+
+        _, full, inv = lax.fori_loop(0, n, column, (gram, jnp.zeros_like(gram), eye))
+        upper_ref[...] = full
         inv_ref[...] = inv
 
 
-def panel_kernel(gram_ref, rows_ref, leg_ref, out_ref, upper_ref, inv_ref):
-    @pl.when(pl.program_id(0) == 0)
-    def _():
-        factorize(gram_ref[...].reshape(128, 128), upper_ref, inv_ref)
-
+def panel_kernel(
+    gram_ref, rows_ref, leg_ref, out_ref, upper_ref, inv_ref, rows, leg, block, rows_sem, leg_sem, out_sem
+):
+    fetch_rows = pltpu.make_async_copy(rows_ref, rows, rows_sem)
+    fetch_rows.start()
+    fetch_leg = [pltpu.make_async_copy(leg_ref.at[j], leg.at[j], leg_sem.at[j]) for j in range(OWN)]
+    for copy in fetch_leg:
+        copy.start()
+    factorize(gram_ref[...].reshape(128, 128), upper_ref, inv_ref)
     hi, lo = split(inv_ref[...])
-    z = mm(hi, rows_ref[0]) + mm(lo, rows_ref[0])
-    z_hi, z_lo = split(z)
     left = lax.broadcasted_iota(jnp.int32, (128, 128), 1) < 64
-    hi_f, lo_f = z_hi.astype(F32), z_lo.astype(F32)
-    cosine = jnp.where(left, hi_f, pltpu.roll(lo_f, 64, axis=1)).astype(BF)
-    sine = jnp.where(left, pltpu.roll(hi_f, 64, axis=1), lo_f).astype(BF)
-    out_ref[0, 0] = mm_nt(leg_ref[0], cosine)
-    out_ref[1, 0] = mm_nt(leg_ref[0], sine)
+    fetch_rows.wait()
+    every = jnp.concatenate([rows[j] for j in range(OWN)], axis=1)
+    z_hi, z_lo = split(mm(hi, every) + mm(lo, every))
+    writes = []
+    for j in range(OWN):
+        cols = slice(j * 128, (j + 1) * 128)
+        hi_f, lo_f = z_hi[:, cols].astype(F32), z_lo[:, cols].astype(F32)
+        cosine = jnp.where(left, hi_f, pltpu.roll(lo_f, 64, axis=1))
+        sine = jnp.where(left, pltpu.roll(hi_f, 64, axis=1), lo_f)
+        weights = jnp.concatenate([cosine, sine], axis=0).astype(BF)
+        fetch_leg[j].wait()
+        for start, stop in ((0, 608), (608, NDEG)):
+            both = mm_nt(leg[j, start:stop, :], weights)
+            block[0, j, start:stop, :] = both[:, :128]
+            block[1, j, start:stop, :] = both[:, 128:]
+        for half in range(2):
+            write = pltpu.make_async_copy(block.at[half, j], out_ref.at[half, j], out_sem.at[half, j])
+            write.start()
+            writes.append(write)
+    for write in writes:
+        write.wait()
 
 
 def panel_stage(gram, rows, turned):
+    any_space = pl.BlockSpec(memory_space=pl.ANY)
     return pl.pallas_call(
         panel_kernel,
         name="panel_stage",
-        grid=(OWN,),
         out_shape=(
             jax.ShapeDtypeStruct((2, OWN, NDEG, 128), F32),
             jax.ShapeDtypeStruct((128, 128), F32),
         ),
-        in_specs=[
-            pl.BlockSpec((NC, 16, 128), lambda j: (0, 0, 0)),
-            pl.BlockSpec((1, 128, 128), lambda j: (j, 0, 0)),
-            pl.BlockSpec((1, NDEG, 128), lambda j: (j, 0, 0)),
+        in_specs=[VM, any_space, any_space],
+        out_specs=(any_space, VM),
+        scratch_shapes=[
+            pltpu.VMEM((128, 128), F32),
+            pltpu.VMEM(rows.shape, BF),
+            pltpu.VMEM(turned.shape, BF),
+            pltpu.VMEM((2, OWN, NDEG, 128), F32),
+            pltpu.SemaphoreType.DMA,
+            pltpu.SemaphoreType.DMA((OWN,)),
+            pltpu.SemaphoreType.DMA((2, OWN)),
         ],
-        out_specs=(
-            pl.BlockSpec((2, 1, NDEG, 128), lambda j: (0, j, 0, 0)),
-            pl.BlockSpec((128, 128), lambda j: (0, 0)),
-        ),
-        scratch_shapes=[pltpu.VMEM((128, 128), F32)],
     )(gram, rows, turned)
 
 

time: 54.7 us -> 52.5 us (0.960)
  Pallas kernels: 53.7 us -> 51.6 us
    pallas_call x1, Pallas kernels: 8.46 us -> 6.36 us  [panel_stage(): pl.pallas_call(panel_kernel, name='panel_stage', out_shape=(jax.ShapeDtyp...]
where the time goes in v5:
time: 52.5 us; the launch traced here: 52.3 us
  Pallas kernels  51.6 us (98%)
  between operations  0.64 us (1%)
    pallas_call x1, Pallas kernels, front_stage(): pl.pallas_call(front_kernel, name='front_stage', out_shape=(jax.ShapeDtyp...  45.3 us
    pallas_call x1, Pallas kernels, panel_stage(): pl.pallas_call(panel_kernel, name='panel_stage', out_shape=(jax.ShapeDtyp...  6.36 us

profile of v5, /device:TPU:1, one launch (start us, length us, event | category | flops | bytes accessed | tf_op | source)
XLA Modules:
  0.0 52.3 jit_solution(6233487057858096492)
XLA Ops:
  0.6 45.3 %front_stage.1 = (bf16[5,128,128]{2,1,0:T(8,128)(2,1)}, f32[8,16,128]{2,1,0:T(8,128)}, bf16[5,1200,128]{2,1,0:T(8,128)(2,1)}) custom-call(bf16[2,80,8,1200]{3,2,1,0:T(8,128)(2,1)} %probes_ref.1, bf16[80,64,1200]{2,1,0:T(8,128)(2,1)} %leg_ref.1, s32[5,128]{1,0:T(8,128)} %bitcast.10, s32[16,24]{1,0:T(8,128)} %bitcast.9, s32[1,16]{1,0:T(1,128)} %count_ref.1, ...), custom_call_target="tpu_custom_call" | custom-call | tf_op jit(solution)/shard_map/front_stage/pallas_call | solution.py:335
  45.9 6.4 %panel_stage.1 = (f32[2,5,1200,128]{3,2,1,0:T(8,128)}, f32[128,128]{1,0:T(8,128)}) custom-call(f32[8,16,128]{2,1,0:T(8,128)} %get-tuple-element.7.gram_ref, bf16[5,128,128]{2,1,0:T(8,128)(2,1)} %get-tuple-element.8.rows_ref, bf16[5,1200,128]{2,1,0:T(8,128)(2,1)} %get-tuple-element.9.leg_ref), custom_call_target="tpu_custom_call" | custom-call | tf_op jit(solution)/shard_map/panel_stage/pallas_call | solution.py:455

commit v6 on v5

--- a/solution.py
+++ b/solution.py
@@ -16,6 +16,8 @@
 OWN = 5
 UNITS = 40
 PIECE = 3
+EARLY = 2
+GROUP = 32
 STEP = 20
 CHUNKS = 4
 
@@ -44,7 +46,7 @@
     rows_out, gram_out, turned_out,
     leg, prob, base, coef, weight, live, hist, norm, part, table, lat_rows, lat_pack, lat_send, lat_recv,
     cos_q, sin_q, cos_b, sin_b, tab_hi, tab_lo, adj_ref, spec_ref, turn_ref, spec, recv, perm, normal,
-    g_part, g_coef, g_track, turned_leg, in_sem, leg_sem, prob_sem, turn_sem, comm, ready,
+    g_part, g_group, g_all, turned_leg, in_sem, leg_sem, prob_sem, turn_sem, comm, ready,
 ):
     c = lax.axis_index("coef")
     t = lax.axis_index("track")
@@ -62,10 +64,10 @@
         pltpu.make_async_copy(ref.at[pl.ds(0, n)], ref.at[pl.ds(0, n)], comm.at[2 * k]).wait()
 
     z, core = lax.div(c, 2), lax.rem(c, 2)
-    y, x = lax.div(t, 4), lax.rem(t, 4)
+    y_chip, x_chip = lax.div(t, 4), lax.rem(t, 4)
     far = (0, 1, 2, 1)
     bands = {(dz, dk): lax.rem(z + dz, 4) * 2 + lax.rem(core + dk, 2) for dz in range(4) for dk in range(2)}
-    tracks = {(dy, dx): lax.rem(y + dy, 4) * 4 + lax.rem(x + dx, 4) for dy in range(4) for dx in range(4)}
+    tracks = {(dy, dx): lax.rem(y_chip + dy, 4) * 4 + lax.rem(x_chip + dx, 4) for dy in range(4) for dx in range(4)}
     steps = [(dz, dk, dy, dx) for dz in range(4) for dk in range(2) for dy in range(4) for dx in range(4)]
     steps.sort(key=lambda d: -(far[d[0]] + far[d[2]] + far[d[3]]) * 2 - d[1])
     peers = [(bands[d[:2]], tracks[d[2:]]) for d in steps if any(d)]
@@ -90,6 +92,24 @@
         pl.semaphore_signal(barrier, 1, device_id=(lax.rem(c + i, NC), t), device_id_type=MESH)
     for i in range(1, NT):
         pl.semaphore_signal(barrier, 1, device_id=(c, lax.rem(t + i, NT)), device_id_type=MESH)
+
+    orders = jnp.concatenate([order_ref[r : r + 1, :] for r in range(OWN)], axis=1)
+    coarse = jnp.broadcast_to(lax.shift_right_logical(orders, 5).astype(F32).astype(BF), (128, ORDERS))
+    fine = jnp.broadcast_to((orders & 31).astype(F32).astype(BF), (128, ORDERS))
+    owner_row = lax.broadcasted_iota(jnp.int32, (128, ORDERS), 0) * OWN
+    slot_lane = lax.broadcasted_iota(jnp.int32, (128, ORDERS), 1)
+    lane = lax.broadcasted_iota(jnp.int32, (128, 128), 1).astype(F32)
+
+    def trig(j, carry):
+        hot = jnp.where(owner_row + j == slot_lane, 1.0, 0.0).astype(BF)
+        order = 32.0 * mm_nt(hot, coarse) + mm_nt(hot, fine)
+        cos_q[j], sin_q[j] = circle(order * lane)
+        cosine, sine = circle(order * (lane * 128.0))
+        cos_b[j] = cosine * (1.0 / math.sqrt(ORDERS))
+        sin_b[j] = sine * (1.0 / math.sqrt(ORDERS))
+        return carry
+
+    lax.fori_loop(0, EARLY, trig, 0)
 
     for copy in small:
         copy.wait()
@@ -157,12 +177,21 @@
         return carry
 
     lax.fori_loop(0, CHUNKS, lat_step, 0)
+    lanes = lax.broadcasted_iota(jnp.int32, (64, 128), 1)
+    slot16 = lax.shift_right_logical(lanes, 4)
+    rest = [jnp.zeros((64, 128), F32)] * 2
     for p in range(8):
-        turned = lat_rows[pl.ds(p, 80, stride=8), :].T
-        for half in range(2):
-            for s in range(NC):
-                start = half * 64 + s * 8
-                lat_pack[s, half, p * 8 : (p + 1) * 8, :] = turned[start : start + 8, :]
+        some = jnp.concatenate([lat_rows[pl.ds(p, 80, stride=8), :], jnp.zeros((48, 128), F32)], axis=0).T
+        cosine, sine = some[:64], some[64:]
+        main = jnp.where(lanes < 64, cosine, pltpu.roll(sine, 64, axis=1))
+        g = p // 2
+        rest[p % 2] = jnp.where(slot16 == 2 * g, pltpu.roll(cosine, (32 * g + 64) % 128, axis=1), rest[p % 2])
+        rest[p % 2] = jnp.where(slot16 == 2 * g + 1, pltpu.roll(sine, (32 * g + 80) % 128, axis=1), rest[p % 2])
+        for s in range(NC):
+            lat_pack[s, p * 8 : (p + 1) * 8, :] = main[s * 8 : (s + 1) * 8, :]
+    for k in range(2):
+        for s in range(NC):
+            lat_pack[s, 64 + k * 8 : 72 + k * 8, :] = rest[k][s * 8 : (s + 1) * 8, :]
     lat_send[...] = lat_pack[...].astype(BF)
     for i in range(1, NC):
         peer = (c + i) % NC
@@ -177,20 +206,7 @@
         peer = (t + i) % NT
         send(table.at[t], table.at[t], 2, c, peer)
 
-    orders = jnp.concatenate([order_ref[r : r + 1, :] for r in range(OWN)], axis=1)
-    coarse = jnp.broadcast_to(lax.shift_right_logical(orders, 5).astype(F32).astype(BF), (128, ORDERS))
-    fine = jnp.broadcast_to((orders & 31).astype(F32).astype(BF), (128, ORDERS))
-    owner_row = lax.broadcasted_iota(jnp.int32, (128, ORDERS), 0) * OWN
-    slot_lane = lax.broadcasted_iota(jnp.int32, (128, ORDERS), 1)
-    lane = lax.broadcasted_iota(jnp.int32, (128, 128), 1).astype(F32)
-
-    def trig(j, carry):
-        hot = jnp.where(owner_row + j == slot_lane, 1.0, 0.0).astype(BF)
-        order = 32.0 * mm_nt(hot, coarse) + mm_nt(hot, fine)
-        cos_q[j], sin_q[j] = circle(order * lane)
-        cosine, sine = circle(order * (lane * 128.0))
-        cos_b[j] = cosine * (1.0 / math.sqrt(ORDERS))
-        sin_b[j] = sine * (1.0 / math.sqrt(ORDERS))
+    def make(j, carry):
         cq, sq, cb, sb = cos_q[j], sin_q[j], cos_b[j], sin_b[j]
         for b in range(10):
             ca, sa = cb[:, b : b + 1], sb[:, b : b + 1]
@@ -203,16 +219,36 @@
             tab_lo[OWN + j, :, cols] = lo
         return carry
 
-    lax.fori_loop(0, OWN, trig, 0)
+    lax.fori_loop(EARLY, OWN, lambda j, carry: make(j, trig(j, carry)), 0)
+    lax.fori_loop(0, EARLY, make, 0)
 
     arrived(lat_recv, NC - 1, 1)
+    slot32 = lax.shift_right_logical(lax.broadcasted_iota(jnp.int32, (16, 128), 1), 5)
+    tail = []
+    for first in (0, 4):
+        parts = [jnp.zeros((16, 128), F32)] * 4
+        for k in range(4):
+            some = lat_recv[first + k, 64:, :].astype(F32)
+            for g in range(4):
+                moved = pltpu.roll(some, (32 * (k - g)) % 128, axis=1) if k != g else some
+                parts[g] = jnp.where(slot32 == k, moved, parts[g])
+        tail.append(jnp.concatenate(parts, axis=0).astype(BF))
+
+    def rows_of(tab, s):
+        own = slice(s * NT, (s + 1) * NT)
+        return [tab[0:4, own, :].reshape(64, NLON), tab[OWN : OWN + 4, own, :].reshape(64, NLON)]
+
+    def rest_of(tab, s):
+        own = slice(s * NT, (s + 1) * NT)
+        return [tab[4, own, :], tab[OWN + 4, own, :]]
+
     grid = jnp.zeros((64, NLON), F32)
-    for s in range(NC):
-        own = slice(s * NT, (s + 1) * NT)
-        for half in range(2):
-            js = slice(half * OWN, (half + 1) * OWN)
-            grid = grid + mm(lat_recv[s, half], tab_hi[js, own, :].reshape(80, NLON))
-            grid = grid + mm(lat_recv[s, half], tab_lo[js, own, :].reshape(80, NLON))
+    for tab in (tab_hi, tab_lo):
+        for s in range(0, NC, 2):
+            pair = jnp.concatenate([lat_recv[s, :64, :], lat_recv[s + 1, :64, :]], axis=1)
+            grid = grid + mm(pair, jnp.concatenate(rows_of(tab, s) + rows_of(tab, s + 1), axis=0))
+        rest_rows = [block for s in range(NC) for block in rest_of(tab, s)]
+        grid = grid + mm(jnp.concatenate(tail, axis=1), jnp.concatenate(rest_rows, axis=0))
     arrived(table, NT - 1, 2)
     for b in range(10):
         x = grid[:, b * 128 : (b + 1) * 128]
@@ -271,44 +307,44 @@
         rows_out[j] = mine
         hi, lo = split(mm(mine, normal[0, j]) + mm(mine, normal[1, j]))
         gram = gram + mm_nt(hi, mine) + mm_nt(lo, mine)
-    g_part[...] = gram.reshape(NC, 16, 128)
+    for k in range(GROUP):
+        g_part[k] = gram[k * 4 : (k + 1) * 4, :]
 
     def turn(j):
         one = leg[t * OWN + j]
         turned_leg[j] = jnp.concatenate([one, one], axis=0).T
         pltpu.make_async_copy(turned_leg.at[j], turned_out.at[j], turn_sem.at[j]).start()
 
-    for i in range(1, NC):
-        peer = (c + i) % NC
-        send(g_part.at[peer], g_coef.at[c], 4, peer, t)
-    g_coef[c] = g_part[c]
+    seat = c * 4 + x_chip
+    for d in steps:
+        if d[2] == 0 and any(d):
+            pc, px = bands[d[:2]], lax.rem(x_chip + d[3], 4)
+            send(g_part.at[pc * 4 + px], g_group.at[seat], 4, pc, y_chip * 4 + px)
+    g_group[seat] = g_part[seat]
     turn(0)
     turn(1)
-    arrived(g_coef, NC - 1, 4)
-    total = g_coef[0]
-    for s in range(1, NC):
-        total = total + g_coef[s]
-    g_track[t] = total
-    for i in range(1, NT):
-        peer = (t + i) % NT
-        send(g_track.at[t], g_track.at[t], 5, c, peer)
+    arrived(g_group, GROUP - 1, 4)
+    total = g_group[0]
+    for k in range(1, GROUP):
+        total = total + g_group[k]
+    mine_at = y_chip * GROUP + seat
+    g_all[mine_at] = total * (1.0 / (2 * ORDERS * NDEG))
+    for pc, pt in peers:
+        send(g_all.at[mine_at], g_all.at[mine_at], 5, pc, pt)
     turn(2)
     turn(3)
-    arrived(g_track, NT - 1, 5)
-    total = g_track[0]
-    for s in range(1, NT):
-        total = total + g_track[s]
-    gram_out[c] = total * (1.0 / (2 * ORDERS * NDEG))
-    for i in range(1, NC):
-        peer = (c + i) % NC
-        send(gram_out.at[c], gram_out.at[c], 6, peer, t)
     turn(4)
-    arrived(gram_out, NC - 1, 6)
+    arrived(g_all, ND - 1, 5)
+    for k in range(GROUP):
+        total = g_all[k]
+        for q in range(1, 4):
+            total = total + g_all[q * GROUP + k]
+        gram_out[k * 4 : (k + 1) * 4, :] = total
     for j in range(OWN):
         pltpu.make_async_copy(turned_leg.at[j], turned_out.at[j], turn_sem.at[j]).wait()
     for ref, n, k in (
         (part, NT - 1, 0), (lat_send, NC - 1, 1), (table, NT - 1, 2), (spec, ND - 1, 3),
-        (g_part, NC - 1, 4), (g_track, NT - 1, 5), (gram_out, NC - 1, 6),
+        (g_part, GROUP - 1, 4), (g_all, ND - 1, 5),
     ):
         sent(ref, n, k)
 
@@ -335,7 +371,7 @@
     return pl.pallas_call(
         front_kernel,
         name="front_stage",
-        out_shape=(jax.ShapeDtypeStruct((OWN, 128, 128), BF), jax.ShapeDtypeStruct((NC, 16, 128), F32),
+        out_shape=(jax.ShapeDtypeStruct((OWN, 128, 128), BF), jax.ShapeDtypeStruct((128, 128), F32),
                    jax.ShapeDtypeStruct((OWN, NDEG, 128), BF)),
         in_specs=[any_space, any_space, VM, VM, VM, any_space, any_space, any_space],
         out_specs=(VM, VM, any_space),
@@ -345,15 +381,15 @@
             vm((slots, 32, 128), F32),
             vm((NT, PIECE, 8, 128), F32), vm((NT, PIECE, 8, 128), F32), vm((NT, PIECE, 8, 128), F32),
             vm((640, 128), F32),
-            vm((NC, 2, 64, 80), F32), vm((NC, 2, 64, 80), BF), vm((NC, 2, 64, 80), BF),
+            vm((NC, 80, 128), F32), vm((NC, 80, 128), BF), vm((NC, 80, 128), BF),
             vm((OWN, 128, 128), F32), vm((OWN, 128, 128), F32), vm((OWN, 128, 128), F32), vm((OWN, 128, 128), F32),
             vm((10, 128, NLON), BF), vm((10, 128, NLON), BF),
             vm((128, NLON), BF), vm((16, 64, 128), F32), vm((1024, 128), F32),
             vm((ND, 8, 128), BF), vm((ND, 8, 128), BF), vm((1024, 640), BF), vm((2, OWN, 128, 128), BF),
-            vm((NC, 16, 128), F32), vm((NC, 16, 128), F32), vm((NT, 16, 128), F32),
+            vm((GROUP, 4, 128), F32), vm((GROUP, 4, 128), F32), vm((ND, 4, 128), F32),
             vm((OWN, NDEG, 128), BF),
             pltpu.SemaphoreType.DMA((3,)), pltpu.SemaphoreType.DMA((CHUNKS,)),
-            pltpu.SemaphoreType.DMA((CHUNKS,)), pltpu.SemaphoreType.DMA((OWN,)), pltpu.SemaphoreType.DMA((14,)),
+            pltpu.SemaphoreType.DMA((CHUNKS,)), pltpu.SemaphoreType.DMA((OWN,)), pltpu.SemaphoreType.DMA((12,)),
             pltpu.SemaphoreType.REGULAR,
         ],
         compiler_params=pltpu.CompilerParams(
@@ -424,7 +460,7 @@
     fetch_leg = [pltpu.make_async_copy(leg_ref.at[j], leg.at[j], leg_sem.at[j]) for j in range(OWN)]
     for copy in fetch_leg:
         copy.start()
-    factorize(gram_ref[...].reshape(128, 128), upper_ref, inv_ref)
+    factorize(gram_ref[...], upper_ref, inv_ref)
     hi, lo = split(inv_ref[...])
     left = lax.broadcasted_iota(jnp.int32, (128, 128), 1) < 64
     fetch_rows.wait()

time: 52.5 us -> 50.7 us (0.966)
  Pallas kernels: 51.6 us -> 49.8 us
    pallas_call x1, Pallas kernels: 45.3 us -> 43.5 us  [front_stage(): pl.pallas_call(front_kernel, name='front_stage', out_shape=(jax.ShapeDtyp...]
where the time goes in v6:
time: 50.7 us; the launch traced here: 50.5 us
  Pallas kernels  49.8 us (98%)
  between operations  0.64 us (1%)
    pallas_call x1, Pallas kernels, front_stage(): pl.pallas_call(front_kernel, name='front_stage', out_shape=(jax.ShapeDtyp...  43.5 us
    pallas_call x1, Pallas kernels, panel_stage(): pl.pallas_call(panel_kernel, name='panel_stage', out_shape=(jax.ShapeDtyp...  6.35 us

profile of v6, /device:TPU:1, one launch (start us, length us, event | category | flops | bytes accessed | tf_op | source)
XLA Modules:
  0.0 50.5 jit_solution(8859742024263765457)
XLA Ops:
  0.6 43.5 %front_stage.1 = (bf16[5,128,128]{2,1,0:T(8,128)(2,1)}, f32[128,128]{1,0:T(8,128)}, bf16[5,1200,128]{2,1,0:T(8,128)(2,1)}) custom-call(bf16[2,80,8,1200]{3,2,1,0:T(8,128)(2,1)} %probes_ref.1, bf16[80,64,1200]{2,1,0:T(8,128)(2,1)} %leg_ref.1, s32[5,128]{1,0:T(8,128)} %bitcast.10, s32[16,24]{1,0:T(8,128)} %bitcast.9, s32[1,16]{1,0:T(1,128)} %count_ref.1, ...), custom_call_target="tpu_custom_call" | custom-call | tf_op jit(solution)/shard_map/front_stage/pallas_call | solution.py:371
  44.1 6.4 %panel_stage.1 = (f32[2,5,1200,128]{3,2,1,0:T(8,128)}, f32[128,128]{1,0:T(8,128)}) custom-call(f32[128,128]{1,0:T(8,128)} %get-tuple-element.7.gram_ref, bf16[5,128,128]{2,1,0:T(8,128)(2,1)} %get-tuple-element.8.rows_ref, bf16[5,1200,128]{2,1,0:T(8,128)(2,1)} %get-tuple-element.9.leg_ref), custom_call_target="tpu_custom_call" | custom-call | tf_op jit(solution)/shard_map/panel_stage/pallas_call | solution.py:491

commit v7 on v6

--- a/solution.py
+++ b/solution.py
@@ -16,7 +16,6 @@
 OWN = 5
 UNITS = 40
 PIECE = 3
-EARLY = 2
 GROUP = 32
 STEP = 20
 CHUNKS = 4
@@ -44,7 +43,7 @@
 def front_kernel(
     probes_ref, leg_ref, order_ref, index_ref, count_ref, base_ref, coef_ref, weight_ref,
     rows_out, gram_out, turned_out,
-    leg, prob, base, coef, weight, live, hist, norm, part, table, lat_rows, lat_pack, lat_send, lat_recv,
+    leg, prob, base, coef, weight, order_map, tile_index, tile_count, rows, live, hist, norm, part, table, lat_rows, lat_pack, lat_send, lat_recv,
     cos_q, sin_q, cos_b, sin_b, tab_hi, tab_lo, adj_ref, spec_ref, turn_ref, spec, recv, perm, normal,
     g_part, g_group, g_all, turned_leg, in_sem, leg_sem, prob_sem, turn_sem, comm, ready,
 ):
@@ -74,7 +73,12 @@
 
     small = [
         pltpu.make_async_copy(src, dst, in_sem.at[k])
-        for k, (src, dst) in enumerate(((base_ref, base), (coef_ref, coef), (weight_ref, weight)))
+        for k, (src, dst) in enumerate(
+            (
+                (base_ref, base), (coef_ref, coef), (weight_ref, weight),
+                (order_ref, order_map), (index_ref, tile_index), (count_ref, tile_count),
+            )
+        )
     ]
     for copy in small:
         copy.start()
@@ -92,24 +96,6 @@
         pl.semaphore_signal(barrier, 1, device_id=(lax.rem(c + i, NC), t), device_id_type=MESH)
     for i in range(1, NT):
         pl.semaphore_signal(barrier, 1, device_id=(c, lax.rem(t + i, NT)), device_id_type=MESH)
-
-    orders = jnp.concatenate([order_ref[r : r + 1, :] for r in range(OWN)], axis=1)
-    coarse = jnp.broadcast_to(lax.shift_right_logical(orders, 5).astype(F32).astype(BF), (128, ORDERS))
-    fine = jnp.broadcast_to((orders & 31).astype(F32).astype(BF), (128, ORDERS))
-    owner_row = lax.broadcasted_iota(jnp.int32, (128, ORDERS), 0) * OWN
-    slot_lane = lax.broadcasted_iota(jnp.int32, (128, ORDERS), 1)
-    lane = lax.broadcasted_iota(jnp.int32, (128, 128), 1).astype(F32)
-
-    def trig(j, carry):
-        hot = jnp.where(owner_row + j == slot_lane, 1.0, 0.0).astype(BF)
-        order = 32.0 * mm_nt(hot, coarse) + mm_nt(hot, fine)
-        cos_q[j], sin_q[j] = circle(order * lane)
-        cosine, sine = circle(order * (lane * 128.0))
-        cos_b[j] = cosine * (1.0 / math.sqrt(ORDERS))
-        sin_b[j] = sine * (1.0 / math.sqrt(ORDERS))
-        return carry
-
-    lax.fori_loop(0, EARLY, trig, 0)
 
     for copy in small:
         copy.wait()
@@ -118,14 +104,14 @@
             copy.start()
     slots, obs = base.shape
     lane16 = lax.broadcasted_iota(jnp.int32, (1, NT), 1)
-    count = jnp.sum(jnp.where(lane16 == t, count_ref[...].astype(F32), 0.0), axis=1, keepdims=True)
+    count = jnp.sum(jnp.where(lane16 == t, tile_count[...].astype(F32), 0.0), axis=1, keepdims=True)
     slot_id = lax.broadcasted_iota(jnp.int32, (slots, obs), 0).astype(F32)
     live[...] = jnp.where(slot_id < count, weight[...], 0.0)
     points = lax.broadcasted_iota(jnp.int32, (128, obs), 0)
 
     def slot(group, carry):
-        for u in range(4):
-            s = group * 4 + u
+        for u in range(12):
+            s = group * 12 + u
             hot = jnp.where(points == base[pl.ds(s, 1), :], 1.0, 0.0).astype(BF)
             four = coef[s].astype(F32)
             eight = jnp.concatenate([four, jnp.zeros_like(four)], axis=0)
@@ -139,16 +125,16 @@
             hist[s] = sums[:32] + sums[32:64] + sums[64:]
         return carry
 
-    lax.fori_loop(0, slots // 4, slot, 0)
+    lax.fori_loop(0, slots // 12, slot, 0)
     diagonals = []
     for d in range(4):
         total = hist[:, 8 * d, :]
         for i in range(1, 4 - d):
             total = total + pltpu.roll(hist[:, 8 * d + i, :], i, axis=1)
         diagonals.append(total)
-    rows = lax.broadcasted_iota(jnp.int32, (80, slots), 0)
-    tile = (rows & 7) * 10 + lax.shift_right_logical(rows, 3)
-    pick = jnp.where(tile == index_ref[pl.ds(t, 1), :], 1.0, 0.0)
+    unit = lax.broadcasted_iota(jnp.int32, (80, slots), 0)
+    tile = (unit & 7) * 10 + lax.shift_right_logical(unit, 3)
+    pick = jnp.where(tile == tile_index[pl.ds(t, 1), :], 1.0, 0.0)
     summed = exact(pick, jnp.concatenate(diagonals, axis=1), NN)
     for u in range(NT * PIECE):
         if u < UNITS:
@@ -206,6 +192,22 @@
         peer = (t + i) % NT
         send(table.at[t], table.at[t], 2, c, peer)
 
+    orders = jnp.concatenate([order_map[r : r + 1, :] for r in range(OWN)], axis=1)
+    coarse = jnp.broadcast_to(lax.shift_right_logical(orders, 5).astype(F32).astype(BF), (128, ORDERS))
+    fine = jnp.broadcast_to((orders & 31).astype(F32).astype(BF), (128, ORDERS))
+    owner_row = lax.broadcasted_iota(jnp.int32, (128, ORDERS), 0) * OWN
+    slot_lane = lax.broadcasted_iota(jnp.int32, (128, ORDERS), 1)
+    lane = lax.broadcasted_iota(jnp.int32, (128, 128), 1).astype(F32)
+
+    def trig(j, carry):
+        hot = jnp.where(owner_row + j == slot_lane, 1.0, 0.0).astype(BF)
+        order = 32.0 * mm_nt(hot, coarse) + mm_nt(hot, fine)
+        cos_q[j], sin_q[j] = circle(order * lane)
+        cosine, sine = circle(order * (lane * 128.0))
+        cos_b[j] = cosine * (1.0 / math.sqrt(ORDERS))
+        sin_b[j] = sine * (1.0 / math.sqrt(ORDERS))
+        return carry
+
     def make(j, carry):
         cq, sq, cb, sb = cos_q[j], sin_q[j], cos_b[j], sin_b[j]
         for b in range(10):
@@ -219,8 +221,7 @@
             tab_lo[OWN + j, :, cols] = lo
         return carry
 
-    lax.fori_loop(EARLY, OWN, lambda j, carry: make(j, trig(j, carry)), 0)
-    lax.fori_loop(0, EARLY, make, 0)
+    lax.fori_loop(0, OWN, lambda j, carry: make(j, trig(j, carry)), 0)
 
     arrived(lat_recv, NC - 1, 1)
     slot32 = lax.shift_right_logical(lax.broadcasted_iota(jnp.int32, (16, 128), 1), 5)
@@ -286,8 +287,8 @@
         one = leg[t * OWN + j]
         two = jnp.concatenate([one, one], axis=0)
         hi, lo = split(jnp.where(same, mm_nt(two, two), 0.0))
-        normal[0, j] = hi
-        normal[1, j] = lo
+        normal[j, :128, :] = hi
+        normal[j, 128:, :] = lo
     row = lax.broadcasted_iota(jnp.int32, (128, 640), 0)
     col = lax.broadcasted_iota(jnp.int32, (128, 640), 1)
     src_i, src_a = lax.shift_right_logical(row, 3), row & 7
@@ -297,16 +298,17 @@
     for s in range(NC):
         perm[s * 128 : (s + 1) * 128, :] = jnp.where(hit & (dst_band == s), 1.0, 0.0).astype(BF)
     arrived(recv, ND - 1, 3)
-    gathered = jnp.zeros((128, 640), F32)
-    for s in range(NC):
-        block = recv[s * NT : (s + 1) * NT].astype(F32).reshape(128, 128).astype(BF)
-        gathered = gathered + mm(block, perm[s * 128 : (s + 1) * 128, :])
-    gram = jnp.zeros((128, 128), F32)
+    blocks = [recv[s * NT : (s + 1) * NT].astype(F32).reshape(128, 128).astype(BF) for s in range(NC)]
+    gathered = mm(jnp.concatenate(blocks, axis=1), perm[...])
+    left, right = [], []
     for j in range(OWN):
         mine = gathered[:, j * 128 : (j + 1) * 128].astype(BF)
-        rows_out[j] = mine
-        hi, lo = split(mm(mine, normal[0, j]) + mm(mine, normal[1, j]))
-        gram = gram + mm_nt(hi, mine) + mm_nt(lo, mine)
+        rows[j] = mine
+        left += split(mm(jnp.concatenate([mine, mine], axis=1), normal[j]))
+        right += [mine, mine]
+    gram = mm_nt(jnp.concatenate(left, axis=1), jnp.concatenate(right, axis=1))
+    keep = pltpu.make_async_copy(rows, rows_out, in_sem.at[6])
+    keep.start()
     for k in range(GROUP):
         g_part[k] = gram[k * 4 : (k + 1) * 4, :]
 
@@ -340,6 +342,7 @@
         for q in range(1, 4):
             total = total + g_all[q * GROUP + k]
         gram_out[k * 4 : (k + 1) * 4, :] = total
+    keep.wait()
     for j in range(OWN):
         pltpu.make_async_copy(turned_leg.at[j], turned_out.at[j], turn_sem.at[j]).wait()
     for ref, n, k in (
@@ -373,11 +376,13 @@
         name="front_stage",
         out_shape=(jax.ShapeDtypeStruct((OWN, 128, 128), BF), jax.ShapeDtypeStruct((128, 128), F32),
                    jax.ShapeDtypeStruct((OWN, NDEG, 128), BF)),
-        in_specs=[any_space, any_space, VM, VM, VM, any_space, any_space, any_space],
-        out_specs=(VM, VM, any_space),
+        in_specs=[any_space] * 8,
+        out_specs=(any_space, VM, any_space),
         scratch_shapes=[
             vm(legendre.shape, BF), vm(probes.shape, BF),
-            vm(base.shape, jnp.int32), vm(coef.shape, BF), vm(weight.shape, F32), vm(weight.shape, F32),
+            vm(base.shape, jnp.int32), vm(coef.shape, BF), vm(weight.shape, F32),
+            vm(orders.shape, jnp.int32), vm(index.shape, jnp.int32), vm(count.shape, jnp.int32),
+            vm((OWN, 128, 128), BF), vm(weight.shape, F32),
             vm((slots, 32, 128), F32),
             vm((NT, PIECE, 8, 128), F32), vm((NT, PIECE, 8, 128), F32), vm((NT, PIECE, 8, 128), F32),
             vm((640, 128), F32),
@@ -385,10 +390,10 @@
             vm((OWN, 128, 128), F32), vm((OWN, 128, 128), F32), vm((OWN, 128, 128), F32), vm((OWN, 128, 128), F32),
             vm((10, 128, NLON), BF), vm((10, 128, NLON), BF),
             vm((128, NLON), BF), vm((16, 64, 128), F32), vm((1024, 128), F32),
-            vm((ND, 8, 128), BF), vm((ND, 8, 128), BF), vm((1024, 640), BF), vm((2, OWN, 128, 128), BF),
+            vm((ND, 8, 128), BF), vm((ND, 8, 128), BF), vm((1024, 640), BF), vm((OWN, 256, 128), BF),
             vm((GROUP, 4, 128), F32), vm((GROUP, 4, 128), F32), vm((ND, 4, 128), F32),
             vm((OWN, NDEG, 128), BF),
-            pltpu.SemaphoreType.DMA((3,)), pltpu.SemaphoreType.DMA((CHUNKS,)),
+            pltpu.SemaphoreType.DMA((7,)), pltpu.SemaphoreType.DMA((CHUNKS,)),
             pltpu.SemaphoreType.DMA((CHUNKS,)), pltpu.SemaphoreType.DMA((OWN,)), pltpu.SemaphoreType.DMA((12,)),
             pltpu.SemaphoreType.REGULAR,
         ],

time: 50.7 us -> 49.2 us (0.970)
  Pallas kernels: 49.8 us -> 48.4 us
    pallas_call x1, Pallas kernels: 43.5 us -> 42 us  [front_stage(): pl.pallas_call(front_kernel, name='front_stage', out_shape=(jax.ShapeDtyp...]
where the time goes in v7:
time: 49.2 us; the launch traced here: 49 us
  Pallas kernels  48.4 us (98%)
  between operations  0.64 us (1%)
    pallas_call x1, Pallas kernels, front_stage(): pl.pallas_call(front_kernel, name='front_stage', out_shape=(jax.ShapeDtyp...  42 us
    pallas_call x1, Pallas kernels, panel_stage(): pl.pallas_call(panel_kernel, name='panel_stage', out_shape=(jax.ShapeDtyp...  6.35 us

profile of v7, /device:TPU:1, one launch (start us, length us, event | category | flops | bytes accessed | tf_op | source)
XLA Modules:
  0.0 49.0 jit_solution(17019060010954294014)
XLA Ops:
  0.6 42.0 %front_stage.1 = (bf16[5,128,128]{2,1,0:T(8,128)(2,1)}, f32[128,128]{1,0:T(8,128)}, bf16[5,1200,128]{2,1,0:T(8,128)(2,1)}) custom-call(bf16[2,80,8,1200]{3,2,1,0:T(8,128)(2,1)} %probes_ref.1, bf16[80,64,1200]{2,1,0:T(8,128)(2,1)} %leg_ref.1, s32[5,128]{1,0:T(8,128)} %bitcast.10, s32[16,24]{1,0:T(8,128)} %bitcast.9, s32[1,16]{1,0:T(1,128)} %count_ref.1, ...), custom_call_target="tpu_custom_call" | custom-call | tf_op jit(solution)/shard_map/front_stage/pallas_call | solution.py:374
  42.7 6.4 %panel_stage.1 = (f32[2,5,1200,128]{3,2,1,0:T(8,128)}, f32[128,128]{1,0:T(8,128)}) custom-call(f32[128,128]{1,0:T(8,128)} %get-tuple-element.7.gram_ref, bf16[5,128,128]{2,1,0:T(8,128)(2,1)} %get-tuple-element.8.rows_ref, bf16[5,1200,128]{2,1,0:T(8,128)(2,1)} %get-tuple-element.9.leg_ref), custom_call_target="tpu_custom_call" | custom-call | tf_op jit(solution)/shard_map/panel_stage/pallas_call | solution.py:496

commit v8 on v7

--- a/solution.py
+++ b/solution.py
@@ -43,9 +43,9 @@
 def front_kernel(
     probes_ref, leg_ref, order_ref, index_ref, count_ref, base_ref, coef_ref, weight_ref,
     rows_out, gram_out, turned_out,
-    leg, prob, base, coef, weight, order_map, tile_index, tile_count, rows, live, hist, norm, part, table, lat_rows, lat_pack, lat_send, lat_recv,
+    leg, prob, base, coef, weight, order_map, tile_index, tile_count, live, hist, norm, part, table, lat_rows, lat_pack, lat_send, lat_recv,
     cos_q, sin_q, cos_b, sin_b, tab_hi, tab_lo, adj_ref, spec_ref, turn_ref, spec, recv, perm, normal,
-    g_part, g_group, g_all, turned_leg, in_sem, leg_sem, prob_sem, turn_sem, comm, ready,
+    g_part, g_group, g_all, in_sem, leg_sem, prob_sem, comm, ready,
 ):
     c = lax.axis_index("coef")
     t = lax.axis_index("track")
@@ -303,19 +303,16 @@
     left, right = [], []
     for j in range(OWN):
         mine = gathered[:, j * 128 : (j + 1) * 128].astype(BF)
-        rows[j] = mine
+        rows_out[j] = mine
         left += split(mm(jnp.concatenate([mine, mine], axis=1), normal[j]))
         right += [mine, mine]
     gram = mm_nt(jnp.concatenate(left, axis=1), jnp.concatenate(right, axis=1))
-    keep = pltpu.make_async_copy(rows, rows_out, in_sem.at[6])
-    keep.start()
     for k in range(GROUP):
         g_part[k] = gram[k * 4 : (k + 1) * 4, :]
 
     def turn(j):
         one = leg[t * OWN + j]
-        turned_leg[j] = jnp.concatenate([one, one], axis=0).T
-        pltpu.make_async_copy(turned_leg.at[j], turned_out.at[j], turn_sem.at[j]).start()
+        turned_out[j] = jnp.concatenate([one, one], axis=0).T
 
     seat = c * 4 + x_chip
     for d in steps:
@@ -342,9 +339,6 @@
         for q in range(1, 4):
             total = total + g_all[q * GROUP + k]
         gram_out[k * 4 : (k + 1) * 4, :] = total
-    keep.wait()
-    for j in range(OWN):
-        pltpu.make_async_copy(turned_leg.at[j], turned_out.at[j], turn_sem.at[j]).wait()
     for ref, n, k in (
         (part, NT - 1, 0), (lat_send, NC - 1, 1), (table, NT - 1, 2), (spec, ND - 1, 3),
         (g_part, GROUP - 1, 4), (g_all, ND - 1, 5),
@@ -377,12 +371,12 @@
         out_shape=(jax.ShapeDtypeStruct((OWN, 128, 128), BF), jax.ShapeDtypeStruct((128, 128), F32),
                    jax.ShapeDtypeStruct((OWN, NDEG, 128), BF)),
         in_specs=[any_space] * 8,
-        out_specs=(any_space, VM, any_space),
+        out_specs=(VM, VM, VM),
         scratch_shapes=[
             vm(legendre.shape, BF), vm(probes.shape, BF),
             vm(base.shape, jnp.int32), vm(coef.shape, BF), vm(weight.shape, F32),
             vm(orders.shape, jnp.int32), vm(index.shape, jnp.int32), vm(count.shape, jnp.int32),
-            vm((OWN, 128, 128), BF), vm(weight.shape, F32),
+            vm(weight.shape, F32),
             vm((slots, 32, 128), F32),
             vm((NT, PIECE, 8, 128), F32), vm((NT, PIECE, 8, 128), F32), vm((NT, PIECE, 8, 128), F32),
             vm((640, 128), F32),
@@ -392,15 +386,14 @@
             vm((128, NLON), BF), vm((16, 64, 128), F32), vm((1024, 128), F32),
             vm((ND, 8, 128), BF), vm((ND, 8, 128), BF), vm((1024, 640), BF), vm((OWN, 256, 128), BF),
             vm((GROUP, 4, 128), F32), vm((GROUP, 4, 128), F32), vm((ND, 4, 128), F32),
-            vm((OWN, NDEG, 128), BF),
-            pltpu.SemaphoreType.DMA((7,)), pltpu.SemaphoreType.DMA((CHUNKS,)),
-            pltpu.SemaphoreType.DMA((CHUNKS,)), pltpu.SemaphoreType.DMA((OWN,)), pltpu.SemaphoreType.DMA((12,)),
+            pltpu.SemaphoreType.DMA((6,)), pltpu.SemaphoreType.DMA((CHUNKS,)),
+            pltpu.SemaphoreType.DMA((CHUNKS,)), pltpu.SemaphoreType.DMA((12,)),
             pltpu.SemaphoreType.REGULAR,
         ],
         compiler_params=pltpu.CompilerParams(
-            collective_id=0, has_side_effects=True, vmem_limit_bytes=56 * 1024 * 1024
+            collective_id=0, has_side_effects=True, vmem_limit_bytes=44 * 1024 * 1024
         ),
-    )(probes, legendre, orders, index, count, base, coef, weight)
+    )(*(pltpu.with_memory_space_constraint(x, pltpu.HBM) for x in (probes, legendre, orders, index, count, base, coef, weight)))
 
 
 def exact(a, b, dims):
@@ -457,19 +450,11 @@
         inv_ref[...] = inv
 
 
-def panel_kernel(
-    gram_ref, rows_ref, leg_ref, out_ref, upper_ref, inv_ref, rows, leg, block, rows_sem, leg_sem, out_sem
-):
-    fetch_rows = pltpu.make_async_copy(rows_ref, rows, rows_sem)
-    fetch_rows.start()
-    fetch_leg = [pltpu.make_async_copy(leg_ref.at[j], leg.at[j], leg_sem.at[j]) for j in range(OWN)]
-    for copy in fetch_leg:
-        copy.start()
+def panel_kernel(gram_ref, rows_ref, leg_ref, out_ref, upper_ref, inv_ref, block, out_sem):
     factorize(gram_ref[...], upper_ref, inv_ref)
     hi, lo = split(inv_ref[...])
     left = lax.broadcasted_iota(jnp.int32, (128, 128), 1) < 64
-    fetch_rows.wait()
-    every = jnp.concatenate([rows[j] for j in range(OWN)], axis=1)
+    every = jnp.concatenate([rows_ref[j] for j in range(OWN)], axis=1)
     z_hi, z_lo = split(mm(hi, every) + mm(lo, every))
     writes = []
     for j in range(OWN):
@@ -478,9 +463,8 @@
         cosine = jnp.where(left, hi_f, pltpu.roll(lo_f, 64, axis=1))
         sine = jnp.where(left, pltpu.roll(hi_f, 64, axis=1), lo_f)
         weights = jnp.concatenate([cosine, sine], axis=0).astype(BF)
-        fetch_leg[j].wait()
         for start, stop in ((0, 608), (608, NDEG)):
-            both = mm_nt(leg[j, start:stop, :], weights)
+            both = mm_nt(leg_ref[j, start:stop, :], weights)
             block[0, j, start:stop, :] = both[:, :128]
             block[1, j, start:stop, :] = both[:, 128:]
         for half in range(2):
@@ -500,17 +484,14 @@
             jax.ShapeDtypeStruct((2, OWN, NDEG, 128), F32),
             jax.ShapeDtypeStruct((128, 128), F32),
         ),
-        in_specs=[VM, any_space, any_space],
+        in_specs=[VM, VM, VM],
         out_specs=(any_space, VM),
         scratch_shapes=[
             pltpu.VMEM((128, 128), F32),
-            pltpu.VMEM(rows.shape, BF),
-            pltpu.VMEM(turned.shape, BF),
             pltpu.VMEM((2, OWN, NDEG, 128), F32),
-            pltpu.SemaphoreType.DMA,
-            pltpu.SemaphoreType.DMA((OWN,)),
             pltpu.SemaphoreType.DMA((2, OWN)),
         ],
+        compiler_params=pltpu.CompilerParams(vmem_limit_bytes=16 * 1024 * 1024),
     )(gram, rows, turned)
 
 

time: 49.2 us -> 47.5 us (0.965)
  Pallas kernels: 48.4 us -> 46.8 us
    pallas_call x1, Pallas kernels: 6.35 us -> 5.4 us  [panel_stage(): pl.pallas_call(panel_kernel, name='panel_stage', out_shape=(jax.ShapeDtyp...]
    pallas_call x1, Pallas kernels: 42 us -> 41.3 us  [front_stage(): pl.pallas_call(front_kernel, name='front_stage', out_shape=(jax.ShapeDtyp...]
where the time goes in v8:
time: 47.5 us; the launch traced here: 47.4 us
  Pallas kernels  46.8 us (99%)
  between operations  0.64 us (1%)
    pallas_call x1, Pallas kernels, front_stage(): pl.pallas_call(front_kernel, name='front_stage', out_shape=(jax.ShapeDtyp...  41.3 us
    pallas_call x1, Pallas kernels, panel_stage(): pl.pallas_call(panel_kernel, name='panel_stage', out_shape=(jax.ShapeDtyp...  5.4 us

profile of v8, /device:TPU:1, one launch (start us, length us, event | category | flops | bytes accessed | tf_op | source)
XLA Modules:
  0.0 47.4 jit_solution(10102816232344511410)
XLA Ops:
  0.6 41.3 %front_stage.1 = (bf16[5,128,128]{2,1,0:T(8,128)(2,1)S(1)}, f32[128,128]{1,0:T(8,128)S(1)}, bf16[5,1200,128]{2,1,0:T(8,128)(2,1)S(1)}) custom-call(bf16[2,80,8,1200]{3,2,1,0:T(8,128)(2,1)} %probes_ref.1, bf16[80,64,1200]{2,1,0:T(8,128)(2,1)} %leg_ref.1, s32[5,128]{1,0:T(8,128)} %bitcast.10, s32[16,24]{1,0:T(8,128)} %bitcast.9, s32[1,16]{1,0:T(1,128)} %count_ref.1, ...), custom_call_target="tpu_custom_call" | custom-call | tf_op jit(solution)/shard_map/front_stage/pallas_call | solution.py:368
  42.0 5.4 %panel_stage.1 = (f32[2,5,1200,128]{3,2,1,0:T(8,128)}, f32[128,128]{1,0:T(8,128)}) custom-call(f32[128,128]{1,0:T(8,128)S(1)} %get-tuple-element.7.gram_ref, bf16[5,128,128]{2,1,0:T(8,128)(2,1)S(1)} %get-tuple-element.8.rows_ref, bf16[5,1200,128]{2,1,0:T(8,128)(2,1)S(1)} %get-tuple-element.9.leg_ref), custom_call_target="tpu_custom_call" | custom-call | tf_op jit(solution)/shard_map/panel_stage/pallas_call | solution.py:480

commit v9 on v8

--- a/solution.py
+++ b/solution.py
@@ -183,14 +183,6 @@
         peer = (c + i) % NC
         send(lat_send.at[peer], lat_recv.at[c], 1, peer, t)
     lat_recv[c] = lat_send[c]
-    arrived(part, NT - 1, 0)
-    total = part[0]
-    for s in range(1, NT):
-        total = total + part[s]
-    table[t] = total
-    for i in range(1, NT):
-        peer = (t + i) % NT
-        send(table.at[t], table.at[t], 2, c, peer)
 
     orders = jnp.concatenate([order_map[r : r + 1, :] for r in range(OWN)], axis=1)
     coarse = jnp.broadcast_to(lax.shift_right_logical(orders, 5).astype(F32).astype(BF), (128, ORDERS))
@@ -221,7 +213,16 @@
             tab_lo[OWN + j, :, cols] = lo
         return carry
 
-    lax.fori_loop(0, OWN, lambda j, carry: make(j, trig(j, carry)), 0)
+    lax.fori_loop(0, 1, lambda j, carry: make(j, trig(j, carry)), 0)
+    arrived(part, NT - 1, 0)
+    total = part[0]
+    for s in range(1, NT):
+        total = total + part[s]
+    table[t] = total
+    for i in range(1, NT):
+        peer = (t + i) % NT
+        send(table.at[t], table.at[t], 2, c, peer)
+    lax.fori_loop(1, OWN, lambda j, carry: make(j, trig(j, carry)), 0)
 
     arrived(lat_recv, NC - 1, 1)
     slot32 = lax.shift_right_logical(lax.broadcasted_iota(jnp.int32, (16, 128), 1), 5)

time: 47.5 us -> 47.4 us (level)
  no operation moved by 1% of the time
where the time goes in v9:
time: 47.4 us; the launch traced here: 47.2 us
  Pallas kernels  46.6 us (98%)
  between operations  0.64 us (1%)
    pallas_call x1, Pallas kernels, front_stage(): pl.pallas_call(front_kernel, name='front_stage', out_shape=(jax.ShapeDtyp...  41.2 us
    pallas_call x1, Pallas kernels, panel_stage(): pl.pallas_call(panel_kernel, name='panel_stage', out_shape=(jax.ShapeDtyp...  5.4 us

profile of v9, /device:TPU:1, one launch (start us, length us, event | category | flops | bytes accessed | tf_op | source)
XLA Modules:
  0.0 47.2 jit_solution(2225198069303720680)
XLA Ops:
  0.6 41.2 %front_stage.1 = (bf16[5,128,128]{2,1,0:T(8,128)(2,1)S(1)}, f32[128,128]{1,0:T(8,128)S(1)}, bf16[5,1200,128]{2,1,0:T(8,128)(2,1)S(1)}) custom-call(bf16[2,80,8,1200]{3,2,1,0:T(8,128)(2,1)} %probes_ref.1, bf16[80,64,1200]{2,1,0:T(8,128)(2,1)} %leg_ref.1, s32[5,128]{1,0:T(8,128)} %bitcast.10, s32[16,24]{1,0:T(8,128)} %bitcast.9, s32[1,16]{1,0:T(1,128)} %count_ref.1, ...), custom_call_target="tpu_custom_call" | custom-call | tf_op jit(solution)/shard_map/front_stage/pallas_call | solution.py:369
  41.8 5.4 %panel_stage.1 = (f32[2,5,1200,128]{3,2,1,0:T(8,128)}, f32[128,128]{1,0:T(8,128)}) custom-call(f32[128,128]{1,0:T(8,128)S(1)} %get-tuple-element.7.gram_ref, bf16[5,128,128]{2,1,0:T(8,128)(2,1)S(1)} %get-tuple-element.8.rows_ref, bf16[5,1200,128]{2,1,0:T(8,128)(2,1)S(1)} %get-tuple-element.9.leg_ref), custom_call_target="tpu_custom_call" | custom-call | tf_op jit(solution)/shard_map/panel_stage/pallas_call | solution.py:481
